TPU v7x, 32 devices: a whole 2x2x4 slice. The times are simulated.
32 devices in a mesh: gx: 8 (over z, x), gy: 4 (over y, core).
Axes of the slice: x: 2, y: 2, z: 4, core: 2. Of those that a mesh axis runs over, the one named last changes fastest.
Arguments:
- fine_cotangent: float32 [2, 128, 1024], P(None, 'gx', 'gy'), may hold values from -6 to 6
- coarse_cotangent: float32 [2, 128, 1024], P(None, 'gx', 'gy'), may hold values from -6 to 6
- upstream_x: int32 [3, 8], replicated, may hold values from -16 to 16, as said below
- upstream_y: int32 [3, 1], replicated, may hold values from -32 to 32, as said below
- fractions: float32 [3, 2], replicated, may hold values from 0.05 to 0.95
Outputs:
- difference: float32 [2, 128, 1024], P(None, 'gx', 'gy')
Inputs may be any that keep to these rules, and one draw needn't show every extreme that they name: `upstream_x`: each entry lies in -16 to 16; both ends occur in every draw. `upstream_y`: each entry lies in -32 to 32; both ends occur in every draw.
All inputs are finite; a program needn't handle non-finite values.
Results may differ from a plain program's by a relative error of at most 0.00002.
Values sent between devices are 32-bit elements; how exact they have to be, the bound alone decides.
No kernel may reach another device: no remote copies, remote signals or barrier semaphores. Data moves between devices by JAX's collectives and lax.ppermute only.
A program may use at most 64 MiB of HBM per device.

v0:
```python
import jax
import jax.numpy as jnp
from jax import lax
from jax.sharding import PartitionSpec as P

LINE = 128
MAXDY = 32


def shifted(block, axis, distance):
    devices = range(lax.axis_size(axis))
    route = [((i - distance) % len(devices), i) for i in devices]
    return lax.ppermute(block, axis, route)


def padded(cells, sides, width):
    for axis, dim in sides:
        count = lax.axis_size(axis)
        head = lax.slice_in_dim(cells, 0, width, axis=dim)
        tail = lax.slice_in_dim(cells, cells.shape[dim] - width, cells.shape[dim], axis=dim)
        cells = jnp.concatenate(
            [
                lax.ppermute(tail, axis, [(i, (i + 1) % count) for i in range(count)]),
                cells,
                lax.ppermute(head, axis, [((i + 1) % count, i) for i in range(count)]),
            ],
            axis=dim,
        )
    return cells


def cubic_weights(fraction):
    position = 1.0 - fraction
    return (
        -position * (position - 1.0) * (position - 2.0) / 6.0,
        (position + 1.0) * (position - 1.0) * (position - 2.0) / 2.0,
        -(position + 1.0) * position * (position - 2.0) / 2.0,
        (position + 1.0) * position * (position - 1.0) / 6.0,
    )


def apply_taps(window, weights, along_axis, length):
    summed = weights[0] * lax.slice_in_dim(window, 3, 3 + length, axis=along_axis)
    for tap_index in range(1, 4):
        summed = summed + weights[tap_index] * lax.slice_in_dim(
            window, 3 - tap_index, 3 - tap_index + length, axis=along_axis
        )
    return summed


def fetch_slab(incoming, offset):
    return shifted(incoming, "gx", offset)


def sweep_x(incoming, shifts, weights):
    level_count, slab_width, row_length = incoming.shape
    blocks = row_length // LINE
    span_devices = min(16, lax.axis_size("gx") // 8)
    local_shifts = lax.dynamic_slice_in_dim(shifts, lax.axis_index("gy") * blocks, blocks)
    rim_cells = (span_devices + 1) * slab_width
    lower_side = [fetch_slab(incoming, distance) for distance in range(span_devices + 1, 0, -1)]
    upper_side = [fetch_slab(incoming, -distance) for distance in range(1, span_devices + 2)]
    extended = jnp.concatenate(lower_side + [incoming] + upper_side, axis=1)
    pieces = []
    for block_index in range(blocks):
        column = lax.slice_in_dim(extended, block_index * LINE, (block_index + 1) * LINE, axis=2)
        window = lax.dynamic_slice_in_dim(
            column, rim_cells + local_shifts[block_index] - 1, slab_width + 3, 1
        )
        pieces.append(apply_taps(window, weights, 1, slab_width))
    return jnp.concatenate(pieces, axis=2)


def sweep_y(incoming, shifts, weights):
    level_count, slab_width, row_length = incoming.shape
    rim_cells = MAXDY + 2
    strip_index = lax.axis_index("gx") * slab_width // LINE
    offset = lax.dynamic_index_in_dim(shifts, strip_index, 0, keepdims=False)
    extended = padded(incoming, (("gy", 2),), rim_cells)
    window = lax.dynamic_slice_in_dim(extended, rim_cells + offset - 1, row_length + 3, 2)
    return apply_taps(window, weights, 2, row_length)


def local(fine_cotangent, coarse_cotangent, upstream_x, upstream_y, fractions):

    def adjoint_pass(incoming, pass_row):
        along_x = cubic_weights(fractions[pass_row, 0])
        along_y = cubic_weights(fractions[pass_row, 1])
        swept = sweep_x(incoming, upstream_x[pass_row], along_x)
        return sweep_y(swept, upstream_y[pass_row], along_y)

    fine_field = adjoint_pass(adjoint_pass(fine_cotangent, 1), 0)
    coarse_field = adjoint_pass(coarse_cotangent, 2)
    return fine_field - coarse_field


def solution(mesh):
    placed = (P(None, "gx", "gy"), P(None, "gx", "gy"), P(), P(), P())
    return jax.shard_map(
        local, mesh=mesh, in_specs=placed, out_specs=P(None, "gx", "gy"), check_vma=False
    )
```

profile of v0, /device:TPU:1, one launch (start us, length us, event | category | flops | bytes accessed | tf_op | source)
XLA Modules:
  0.0 67.3 jit_solution(8657479839350391111)
XLA Ops:
  0.0 2.1 %collective-permute-start = (f32[2,16,256]{2,1,0:T(8,128)}, f32[2,16,256]{2,1,0:T(8,128)S(1)}, u32[]{:S(2)}, u32[]{:S(2)}) collective-permute-start(f32[2,16,256]{2,1,0:T(8,128)} %param.5), channel_id=1, source_target_pairs={{24,0},{28,4},{0,8},{4,12},{8,16},{12,20},{16,24},{20,28},{25,1},{... | collective-permute-start | bytes 98312 | tf_op jit(solution)/shard_map/ppermute | solution.py:13
  2.1 1.2 %collective-permute-start.1 = (f32[2,16,256]{2,1,0:T(8,128)}, f32[2,16,256]{2,1,0:T(8,128)S(1)}, u32[]{:S(2)}, u32[]{:S(2)}) collective-permute-start(f32[2,16,256]{2,1,0:T(8,128)} %param.5), channel_id=1, source_target_pairs={{28,0},{0,4},{4,8},{8,12},{12,16},{16,20},{20,24},{24,28},{29,1},{... | collective-permute-start | bytes 98312 | tf_op jit(solution)/shard_map/ppermute | solution.py:13
  3.3 3.0 %collective-permute-start.2 = (f32[2,16,256]{2,1,0:T(8,128)}, f32[2,16,256]{2,1,0:T(8,128)S(1)}, u32[]{:S(2)}, u32[]{:S(2)}) collective-permute-start(f32[2,16,256]{2,1,0:T(8,128)} %param.5), channel_id=1, source_target_pairs={{4,0},{8,4},{12,8},{16,12},{20,16},{24,20},{28,24},{0,28},{5,1},{9... | collective-permute-start | bytes 98312 | tf_op jit(solution)/shard_map/ppermute | solution.py:13
  6.3 0.3 collective-permute-start.3
  6.5 1.2 %collective-permute-start.12 = (f32[2,16,256]{2,1,0:T(8,128)}, f32[2,16,256]{2,1,0:T(8,128)S(1)}, u32[]{:S(2)}, u32[]{:S(2)}) collective-permute-start(f32[2,16,256]{2,1,0:T(8,128)} %param.6), channel_id=1, source_target_pairs={{24,0},{28,4},{0,8},{4,12},{8,16},{12,20},{16,24},{20,28},{25,1},{... | collective-permute-start | bytes 98312 | tf_op jit(solution)/shard_map/ppermute | solution.py:13
  7.7 0.7 %copy-done.4 = s32[3,8]{1,0:T(4,128)S(1)} copy-done((s32[3,8]{1,0:T(4,128)S(1)}, s32[3,8]{1,0:T(4,128)}, u32[]{:S(2)}) %copy-start.4) | copy-done | bytes 120
  8.4 0.1 constant_dynamic-slice_fusion.2
  8.5 0.6 fusion.34
  9.2 0.0 copy-done.2
  9.2 0.7 fusion.32
  9.8 0.6 fusion.35
  10.5 0.1 constant_dynamic-slice_fusion
  10.6 0.6 fusion.33
  11.2 0.6 fusion.36
  38.0 0.0 copy-start.1
  38.1 0.0 collective-permute-done
  38.1 0.7 %copy-done.1 = f32[2,16,256]{2,1,0:T(8,128)S(1)} copy-done((f32[2,16,256]{2,1,0:T(8,128)S(1)}, f32[2,16,256]{2,1,0:T(8,128)}, u32[]{:S(2)}) %copy-start.1) | copy-done | bytes 32792
  38.7 0.0 collective-permute-start.13
  38.8 0.0 collective-permute-done.1
  38.8 4.2 %collective-permute-start.14 = (f32[2,16,256]{2,1,0:T(8,128)S(1)}, f32[2,16,256]{2,1,0:T(8,128)S(1)}, u32[]{:S(2)}, u32[]{:S(2)}) collective-permute-start(f32[2,16,256]{2,1,0:T(8,128)S(1)} %copy-done.1), channel_id=1, source_target_pairs={{4,0},{8,4},{12,8},{16,12},{20,16},{24,20},{28,24},{0,28},{5,1},{9... | collective-permute-start | bytes 98312 | tf_op jit(solution)/shard_map/ppermute | solution.py:13
  43.0 0.0 collective-permute-done.2
  43.0 0.3 collective-permute-start.15
  43.3 0.0 collective-permute-done.3
  43.4 0.1 slice.271
  43.5 4.0 %collective-permute-start.4 = (f32[2,16,34]{2,1,0:T(8,128)S(1)}, f32[2,16,34]{2,1,0:T(8,128)S(1)}, u32[]{:S(2)}, u32[]{:S(2)}) collective-permute-start(f32[2,16,34]{2,1,0:T(8,128)S(1)} %slice.271), channel_id=1, source_target_pairs={{0,1},{1,2},{2,3},{3,0},{4,5},{5,6},{6,7},{7,4},{8,9},{9,10},{10,1... | collective-permute-start | bytes 13064 | tf_op jit(solution)/shard_map/ppermute | solution.py:23
  47.4 0.1 collective-permute-start.5
  47.6 0.0 collective-permute-done.15
  47.7 0.1 slice.287
  47.7 3.1 %collective-permute-start.16 = (f32[2,16,34]{2,1,0:T(8,128)S(1)}, f32[2,16,34]{2,1,0:T(8,128)S(1)}, u32[]{:S(2)}, u32[]{:S(2)}) collective-permute-start(f32[2,16,34]{2,1,0:T(8,128)S(1)} %slice.287), channel_id=1, source_target_pairs={{0,1},{1,2},{2,3},{3,0},{4,5},{5,6},{6,7},{7,4},{8,9},{9,10},{10,1... | collective-permute-start | bytes 13064 | tf_op jit(solution)/shard_map/ppermute | solution.py:23
  50.9 0.1 dynamic-slice_maximum_fusion.6
  51.0 0.1 fusion.7
  51.1 1.5 %collective-permute-start.6 = (f32[2,16,256]{2,1,0:T(8,128)S(1)}, f32[2,16,256]{2,1,0:T(8,128)S(1)}, u32[]{:S(2)}, u32[]{:S(2)}) collective-permute-start(f32[2,16,256]{2,1,0:T(8,128)S(1)} %fusion.7), channel_id=1, source_target_pairs={{24,0},{28,4},{0,8},{4,12},{8,16},{12,20},{16,24},{20,28},{25,1},{... | collective-permute-start | bytes 98312 | tf_op jit(solution)/shard_map/ppermute | solution.py:13
  52.6 0.1 collective-permute-start.17
  52.6 0.1 collective-permute-start.7
  52.7 4.1 %collective-permute-start.8 = (f32[2,16,256]{2,1,0:T(8,128)S(1)}, f32[2,16,256]{2,1,0:T(8,128)S(1)}, u32[]{:S(2)}, u32[]{:S(2)}) collective-permute-start(f32[2,16,256]{2,1,0:T(8,128)S(1)} %fusion.7), channel_id=1, source_target_pairs={{4,0},{8,4},{12,8},{16,12},{20,16},{24,20},{28,24},{0,28},{5,1},{9... | collective-permute-start | bytes 98312 | tf_op jit(solution)/shard_map/ppermute | solution.py:13
  56.9 0.1 collective-permute-start.9
  56.9 1.3 %collective-permute-done.7 = f32[2,16,256]{2,1,0:T(8,128)S(1)} collective-permute-done((f32[2,16,256]{2,1,0:T(8,128)S(1)}, f32[2,16,256]{2,1,0:T(8,128)S(1)}, u32[]{:S(2)}, u32[]{:S(2)}) %collective-permute-start.7) | collective-permute-done | bytes 32800 | tf_op jit(solution)/shard_map/ppermute | solution.py:13
  58.2 0.1 constant_dynamic-update-slice_fusion.7
  58.3 1.3 %collective-permute-done.9 = f32[2,16,256]{2,1,0:T(8,128)S(1)} collective-permute-done((f32[2,16,256]{2,1,0:T(8,128)S(1)}, f32[2,16,256]{2,1,0:T(8,128)S(1)}, u32[]{:S(2)}, u32[]{:S(2)}) %collective-permute-start.9) | collective-permute-done | bytes 32800 | tf_op jit(solution)/shard_map/ppermute | solution.py:13
  59.7 0.1 slice.279
  59.8 3.4 %collective-permute-start.10 = (f32[2,16,34]{2,1,0:T(8,128)S(1)}, f32[2,16,34]{2,1,0:T(8,128)S(1)}, u32[]{:S(2)}, u32[]{:S(2)}) collective-permute-start(f32[2,16,34]{2,1,0:T(8,128)S(1)} %slice.279), channel_id=1, source_target_pairs={{0,1},{1,2},{2,3},{3,0},{4,5},{5,6},{6,7},{7,4},{8,9},{9,10},{10,1... | collective-permute-start | bytes 13064 | tf_op jit(solution)/shard_map/ppermute | solution.py:23
  63.2 0.1 collective-permute-start.11
  63.2 0.0 collective-permute-done.16
  63.3 0.1 dynamic-slice_maximum_fusion
  63.4 0.6 collective-permute-done.10
  64.0 2.4 %collective-permute-done.11 = f32[2,16,34]{2,1,0:T(8,128)S(1)} collective-permute-done((f32[2,16,34]{2,1,0:T(8,128)S(1)}, f32[2,16,34]{2,1,0:T(8,128)S(1)}, u32[]{:S(2)}, u32[]{:S(2)}) %collective-permute-start.11) | collective-permute-done | bytes 4384 | tf_op jit(solution)/shard_map/ppermute | solution.py:25
  66.4 0.1 dynamic-slice_maximum_fusion.3
  66.5 0.7 %fusion.1 = f32[2,16,256]{2,1,0:T(8,128)} fusion(f32[2,16,259]{2,1,0:T(8,128)S(1)} %dynamic-slice_maximum_fusion, f32[2,16,259]{2,1,0:T(8,128)S(1)} %dynamic-slice_maximum_fusion.3, f32[]{:T(128)S(6)} %div.99, f32[]{:T(128)S(6)} %div.98, f32[]{:T(128)S(6)} %div.97, f32[]{:T(128)S(6)} %div.92, f32[]{:T(128)S(6)} %div.91, f32[]{:T(128)S(6)} %div.90, ...), kind=kLoop, calls=%fused_computation.11 | loop fusion | flops 122880 | bytes 294944 | tf_op jit(solution)/shard_map/sub | solution.py:94
  (38 shorter events, 0.3 us)
Async XLA Ops:
  0.0 38.1 %collective-permute-start = (f32[2,16,256]{2,1,0:T(8,128)}, f32[2,16,256]{2,1,0:T(8,128)S(1)}, u32[]{:S(2)}, u32[]{:S(2)}) collective-permute-start(f32[2,16,256]{2,1,0:T(8,128)} %param.5), channel_id=1, source_target_pairs={{24,0},{28,4},{0,8},{4,12},{8,16},{12,20},{16,24},{20,28},{25,1},{... | collective-permute-start | bytes 98312 | tf_op jit(solution)/shard_map/ppermute | solution.py:13
  2.1 36.6 %collective-permute-start.1 = (f32[2,16,256]{2,1,0:T(8,128)}, f32[2,16,256]{2,1,0:T(8,128)S(1)}, u32[]{:S(2)}, u32[]{:S(2)}) collective-permute-start(f32[2,16,256]{2,1,0:T(8,128)} %param.5), channel_id=1, source_target_pairs={{28,0},{0,4},{4,8},{8,12},{12,16},{16,20},{20,24},{24,28},{29,1},{... | collective-permute-start | bytes 98312 | tf_op jit(solution)/shard_map/ppermute | solution.py:13
  3.3 39.7 %collective-permute-start.2 = (f32[2,16,256]{2,1,0:T(8,128)}, f32[2,16,256]{2,1,0:T(8,128)S(1)}, u32[]{:S(2)}, u32[]{:S(2)}) collective-permute-start(f32[2,16,256]{2,1,0:T(8,128)} %param.5), channel_id=1, source_target_pairs={{4,0},{8,4},{12,8},{16,12},{20,16},{24,20},{28,24},{0,28},{5,1},{9... | collective-permute-start | bytes 98312 | tf_op jit(solution)/shard_map/ppermute | solution.py:13
  6.3 37.0 %collective-permute-start.3 = (f32[2,16,256]{2,1,0:T(8,128)}, f32[2,16,256]{2,1,0:T(8,128)S(1)}, u32[]{:S(2)}, u32[]{:S(2)}) collective-permute-start(f32[2,16,256]{2,1,0:T(8,128)} %param.5), channel_id=1, source_target_pairs={{8,0},{12,4},{16,8},{20,12},{24,16},{28,20},{0,24},{4,28},{9,1},{1... | collective-permute-start | bytes 98312 | tf_op jit(solution)/shard_map/ppermute | solution.py:13
  6.5 40.9 %collective-permute-start.12 = (f32[2,16,256]{2,1,0:T(8,128)}, f32[2,16,256]{2,1,0:T(8,128)S(1)}, u32[]{:S(2)}, u32[]{:S(2)}) collective-permute-start(f32[2,16,256]{2,1,0:T(8,128)} %param.6), channel_id=1, source_target_pairs={{24,0},{28,4},{0,8},{4,12},{8,16},{12,20},{16,24},{20,28},{25,1},{... | collective-permute-start | bytes 98312 | tf_op jit(solution)/shard_map/ppermute | solution.py:13
  7.7 0.7 %copy-start.4 = (s32[3,8]{1,0:T(4,128)S(1)}, s32[3,8]{1,0:T(4,128)}, u32[]{:S(2)}) copy-start(s32[3,8]{1,0:T(4,128)} %param.7) | copy-start | bytes 292
  8.5 0.7 %copy-start.2 = (f32[3,2]{0,1:T(2,128)S(1)}, f32[3,2]{0,1:T(2,128)}, u32[]{:S(2)}) copy-start(f32[3,2]{0,1:T(2,128)} %param.9) | copy-start | bytes 76
  9.2 0.7 copy-start.3
  38.0 0.8 %copy-start.1 = (f32[2,16,256]{2,1,0:T(8,128)S(1)}, f32[2,16,256]{2,1,0:T(8,128)}, u32[]{:S(2)}) copy-start(f32[2,16,256]{2,1,0:T(8,128)} %param.6) | copy-start | bytes 98308
  38.7 8.8 %collective-permute-start.13 = (f32[2,16,256]{2,1,0:T(8,128)S(1)}, f32[2,16,256]{2,1,0:T(8,128)S(1)}, u32[]{:S(2)}, u32[]{:S(2)}) collective-permute-start(f32[2,16,256]{2,1,0:T(8,128)S(1)} %copy-done.1), channel_id=1, source_target_pairs={{28,0},{0,4},{4,8},{8,12},{12,16},{16,20},{20,24},{24,28},{29,1},{... | collective-permute-start | bytes 98312 | tf_op jit(solution)/shard_map/ppermute | solution.py:13
  38.8 4.2 %copy-start = (f32[2,16,256]{2,1,0:T(8,128)S(1)}, f32[2,16,256]{2,1,0:T(8,128)}, u32[]{:S(2)}) copy-start(f32[2,16,256]{2,1,0:T(8,128)} %param.5) | copy-start | bytes 98308
  38.8 8.8 %collective-permute-start.14 = (f32[2,16,256]{2,1,0:T(8,128)S(1)}, f32[2,16,256]{2,1,0:T(8,128)S(1)}, u32[]{:S(2)}, u32[]{:S(2)}) collective-permute-start(f32[2,16,256]{2,1,0:T(8,128)S(1)} %copy-done.1), channel_id=1, source_target_pairs={{4,0},{8,4},{12,8},{16,12},{20,16},{24,20},{28,24},{0,28},{5,1},{9... | collective-permute-start | bytes 98312 | tf_op jit(solution)/shard_map/ppermute | solution.py:13
  43.0 4.6 %collective-permute-start.15 = (f32[2,16,256]{2,1,0:T(8,128)S(1)}, f32[2,16,256]{2,1,0:T(8,128)S(1)}, u32[]{:S(2)}, u32[]{:S(2)}) collective-permute-start(f32[2,16,256]{2,1,0:T(8,128)S(1)} %copy-done.1), channel_id=1, source_target_pairs={{8,0},{12,4},{16,8},{20,12},{24,16},{28,20},{0,24},{4,28},{9,1},{1... | collective-permute-start | bytes 98312 | tf_op jit(solution)/shard_map/ppermute | solution.py:13
  43.5 7.4 %collective-permute-start.4 = (f32[2,16,34]{2,1,0:T(8,128)S(1)}, f32[2,16,34]{2,1,0:T(8,128)S(1)}, u32[]{:S(2)}, u32[]{:S(2)}) collective-permute-start(f32[2,16,34]{2,1,0:T(8,128)S(1)} %slice.271), channel_id=1, source_target_pairs={{0,1},{1,2},{2,3},{3,0},{4,5},{5,6},{6,7},{7,4},{8,9},{9,10},{10,1... | collective-permute-start | bytes 13064 | tf_op jit(solution)/shard_map/ppermute | solution.py:23
  47.4 3.4 %collective-permute-start.5 = (f32[2,16,34]{2,1,0:T(8,128)S(1)}, f32[2,16,34]{2,1,0:T(8,128)S(1)}, u32[]{:S(2)}, u32[]{:S(2)}) collective-permute-start(f32[2,16,34]{2,1,0:T(8,128)S(1)} %bitcast.46), channel_id=1, source_target_pairs={{1,0},{2,1},{3,2},{0,3},{5,4},{6,5},{7,6},{4,7},{9,8},{10,9},{11,1... | collective-permute-start | bytes 13064 | tf_op jit(solution)/shard_map/ppermute | solution.py:25
  47.7 15.5 %collective-permute-start.16 = (f32[2,16,34]{2,1,0:T(8,128)S(1)}, f32[2,16,34]{2,1,0:T(8,128)S(1)}, u32[]{:S(2)}, u32[]{:S(2)}) collective-permute-start(f32[2,16,34]{2,1,0:T(8,128)S(1)} %slice.287), channel_id=1, source_target_pairs={{0,1},{1,2},{2,3},{3,0},{4,5},{5,6},{6,7},{7,4},{8,9},{9,10},{10,1... | collective-permute-start | bytes 13064 | tf_op jit(solution)/shard_map/ppermute | solution.py:23
  51.1 5.8 %collective-permute-start.6 = (f32[2,16,256]{2,1,0:T(8,128)S(1)}, f32[2,16,256]{2,1,0:T(8,128)S(1)}, u32[]{:S(2)}, u32[]{:S(2)}) collective-permute-start(f32[2,16,256]{2,1,0:T(8,128)S(1)} %fusion.7), channel_id=1, source_target_pairs={{24,0},{28,4},{0,8},{4,12},{8,16},{12,20},{16,24},{20,28},{25,1},{... | collective-permute-start | bytes 98312 | tf_op jit(solution)/shard_map/ppermute | solution.py:13
  52.6 10.7 %collective-permute-start.17 = (f32[2,16,34]{2,1,0:T(8,128)S(1)}, f32[2,16,34]{2,1,0:T(8,128)S(1)}, u32[]{:S(2)}, u32[]{:S(2)}) collective-permute-start(f32[2,16,34]{2,1,0:T(8,128)S(1)} %bitcast.45), channel_id=1, source_target_pairs={{1,0},{2,1},{3,2},{0,3},{5,4},{6,5},{7,6},{4,7},{9,8},{10,9},{11,1... | collective-permute-start | bytes 13064 | tf_op jit(solution)/shard_map/ppermute | solution.py:25
  52.6 5.5 %collective-permute-start.7 = (f32[2,16,256]{2,1,0:T(8,128)S(1)}, f32[2,16,256]{2,1,0:T(8,128)S(1)}, u32[]{:S(2)}, u32[]{:S(2)}) collective-permute-start(f32[2,16,256]{2,1,0:T(8,128)S(1)} %fusion.7), channel_id=1, source_target_pairs={{28,0},{0,4},{4,8},{8,12},{12,16},{16,20},{20,24},{24,28},{29,1},{... | collective-permute-start | bytes 98312 | tf_op jit(solution)/shard_map/ppermute | solution.py:13
  52.7 5.6 %collective-permute-start.8 = (f32[2,16,256]{2,1,0:T(8,128)S(1)}, f32[2,16,256]{2,1,0:T(8,128)S(1)}, u32[]{:S(2)}, u32[]{:S(2)}) collective-permute-start(f32[2,16,256]{2,1,0:T(8,128)S(1)} %fusion.7), channel_id=1, source_target_pairs={{4,0},{8,4},{12,8},{16,12},{20,16},{24,20},{28,24},{0,28},{5,1},{9... | collective-permute-start | bytes 98312 | tf_op jit(solution)/shard_map/ppermute | solution.py:13
  56.9 2.8 %collective-permute-start.9 = (f32[2,16,256]{2,1,0:T(8,128)S(1)}, f32[2,16,256]{2,1,0:T(8,128)S(1)}, u32[]{:S(2)}, u32[]{:S(2)}) collective-permute-start(f32[2,16,256]{2,1,0:T(8,128)S(1)} %fusion.7), channel_id=1, source_target_pairs={{8,0},{12,4},{16,8},{20,12},{24,16},{28,20},{0,24},{4,28},{9,1},{1... | collective-permute-start | bytes 98312 | tf_op jit(solution)/shard_map/ppermute | solution.py:13
  59.8 4.3 %collective-permute-start.10 = (f32[2,16,34]{2,1,0:T(8,128)S(1)}, f32[2,16,34]{2,1,0:T(8,128)S(1)}, u32[]{:S(2)}, u32[]{:S(2)}) collective-permute-start(f32[2,16,34]{2,1,0:T(8,128)S(1)} %slice.279), channel_id=1, source_target_pairs={{0,1},{1,2},{2,3},{3,0},{4,5},{5,6},{6,7},{7,4},{8,9},{9,10},{10,1... | collective-permute-start | bytes 13064 | tf_op jit(solution)/shard_map/ppermute | solution.py:23
  63.2 3.2 %collective-permute-start.11 = (f32[2,16,34]{2,1,0:T(8,128)S(1)}, f32[2,16,34]{2,1,0:T(8,128)S(1)}, u32[]{:S(2)}, u32[]{:S(2)}) collective-permute-start(f32[2,16,34]{2,1,0:T(8,128)S(1)} %bitcast.47), channel_id=1, source_target_pairs={{1,0},{2,1},{3,2},{0,3},{5,4},{6,5},{7,6},{4,7},{9,8},{10,9},{11,1... | collective-permute-start | bytes 13064 | tf_op jit(solution)/shard_map/ppermute | solution.py:25
where the time goes:
time: 67.9 us; the launch traced here: 67.3 us
  starting transfers between devices  28.6 us (42%)
  between operations  26.6 us (39%)
  waiting for transfers between devices  5.62 us (8%)
  local copies, waits for them, and re-layouts  5.01 us (7%)
  other arithmetic  1.43 us (2%)
    ppermute x12, starting transfers between devices, shifted(): return lax.ppermute(block, axis, route)  18 us
    ppermute x3, starting transfers between devices, padded(): lax.ppermute(tail, axis, [(i, (i + 1) % count) for i in range(count)])  10.5 us
    ppermute x12, waiting for transfers between devices, shifted(): return lax.ppermute(block, axis, route)  2.61 us
    ppermute x3, waiting for transfers between devices, padded(): lax.ppermute(head, axis, [((i + 1) % count, i) for i in range(count)])  2.37 us
    slice x3, local copies, waits for them, and re-layouts, sweep_x(): local_shifts[block_index]  1.83 us
    unnamed x21, local copies, waits for them, and re-layouts  1.46 us
  transfers between devices with their start and end apart: 18, of which 4 were waited for; matrix products, arithmetic and copies ran while one was open for 6% of the time, Pallas kernels for 0%

commit v1 on v0

v1 whole, which is shorter than its diff:
```python
import functools

import jax
import jax.numpy as jnp
from jax import lax
from jax.experimental import pallas as pl
from jax.experimental.pallas import tpu as pltpu
from jax.sharding import PartitionSpec as P

LINE = 128
MAXDY = 32
EDGE = 8


def rounded(rows):
    return -(-rows // EDGE) * EDGE


def shifted(block, axis, distance):
    count = lax.axis_size(axis)
    return lax.ppermute(block, axis, [((i - distance) % count, i) for i in range(count)])


def ring_window(block, slabs):
    lower = [shifted(block, "gx", distance) for distance in range(slabs, 0, -1)]
    upper = [shifted(block, "gx", -distance) for distance in range(1, slabs + 1)]
    return jnp.concatenate(lower + [block] + upper, axis=1)


def cubic_weights(fraction):
    position = 1.0 - fraction
    return (
        -position * (position - 1.0) * (position - 2.0) * (1.0 / 6.0),
        (position + 1.0) * (position - 1.0) * (position - 2.0) * 0.5,
        -(position + 1.0) * position * (position - 2.0) * 0.5,
        (position + 1.0) * position * (position - 1.0) * (1.0 / 6.0),
    )


def weighted(weights, term):
    summed = weights[0] * term(0)
    for tap in range(1, 4):
        summed = summed + weights[tap] * term(tap)
    return summed


def sweep_x_kernel(slab, center_fine, center_coarse,
                   shifts, fractions, fine, coarse, own, own_coarse, to_left, to_right,
                   fine_lines, coarse_lines):
    levels = fine.shape[0]
    lines = own.shape[0]
    rows = own.shape[3]
    total = shifts.shape[1]
    first = lax.axis_index("gy") * lines
    fine_weights = cubic_weights(fractions[1, 0])
    coarse_weights = cubic_weights(fractions[2, 0])
    for line in range(lines):
        lanes = slice(line * LINE, (line + 1) * LINE)
        fine_lines[line] = fine[:, :, lanes]
        coarse_lines[line] = coarse[:, :, lanes]
        inner = shifts[1, first + line]
        for slot in range(3):
            region = lax.rem(first + line + slot - 1 + total, total)
            start = center_fine - 1 + inner + shifts[0, region]
            for level in range(levels):
                summed = weighted(
                    fine_weights,
                    lambda tap: fine_lines[line, level, pl.ds(start + 2 - tap, rows)],
                )
                own[line, slot, level] = summed
                if line == 0 and slot < 2:
                    to_left[level, slot * rows:(slot + 1) * rows] = summed
                if line == lines - 1 and slot > 0:
                    to_right[level, (slot - 1) * rows:slot * rows] = summed
        start = center_coarse + shifts[2, first + line]
        for level in range(levels):
            summed = weighted(
                coarse_weights,
                lambda tap: coarse_lines[line, level, pl.ds(start + 2 - tap, slab)],
            )
            own_coarse[line, level] = summed
            if line == 0:
                to_left[level, 2 * rows:] = summed
            if line == lines - 1:
                to_right[level, 2 * rows:] = summed


def turned(weights, offset, current, left, right, lane):
    beside = jnp.where(lane < LINE // 2, right, left)

    def term(tap):
        distance = offset + 2 - tap
        outside = (lane < distance) | (lane >= LINE + distance)
        mixed = jnp.where(outside, beside, current)
        return pltpu.roll(mixed, lax.rem(LINE - distance, LINE), 1)

    return weighted(weights, term)


def sweep_y_kernel(shifts_x, shifts_y, fractions, own, own_coarse, from_left, from_right,
                   out, held):
    lines, _, levels, rows, _ = own.shape
    slab = own_coarse.shape[2]
    total = shifts_x.shape[1]
    strips = shifts_y.shape[1]
    first = lax.axis_index("gy") * lines
    base = lax.axis_index("gx") * slab
    extent = lax.axis_size("gx") * slab
    outer_x = cubic_weights(fractions[0, 0])
    outer_y = cubic_weights(fractions[0, 1])
    inner_y = cubic_weights(fractions[1, 1])
    coarse_y = cubic_weights(fractions[2, 1])
    tall = lax.broadcasted_iota(jnp.int32, (rows, LINE), 1)
    flat = lax.broadcasted_iota(jnp.int32, (slab, LINE), 1)
    strip = lax.div(base, LINE)

    def pieces(region, level):
        if region < 0:
            current = from_left[level, 0:rows]
            return current, current, own[0, 0, level]
        if region == lines:
            current = from_right[level, rows:2 * rows]
            return current, own[lines - 1, 2, level], current
        left = own[region - 1, 2, level] if region else from_left[level, rows:2 * rows]
        right = own[region + 1, 0, level] if region < lines - 1 else from_right[level, 0:rows]
        return own[region, 1, level], left, right

    outer = {}
    for region in range(-1, lines + 1):
        if strips > 1:
            shift = shifts_x[0, lax.rem(first + region + total, total)]
            start = lax.rem(base + shift - 1 + extent, extent)
            here = lax.div(start, LINE)
            after = lax.rem(here + 1, strips)
            row = lax.broadcasted_iota(jnp.int32, (rows, LINE), 0)
            beyond = row >= LINE - lax.rem(start, LINE)
        for level in range(levels):
            current, left, right = pieces(region, level)
            if strips > 1:
                swept = jnp.where(
                    beyond,
                    turned(inner_y, shifts_y[1, after], current, left, right, tall),
                    turned(inner_y, shifts_y[1, here], current, left, right, tall),
                )
            else:
                swept = turned(inner_y, shifts_y[1, 0], current, left, right, tall)
            held[region + 1, level] = swept
            outer[region, level] = weighted(
                outer_x, lambda tap: held[region + 1, level, 3 - tap:3 - tap + slab]
            )
    for line in range(lines):
        for level in range(levels):
            fine_field = turned(
                outer_y, shifts_y[0, strip], outer[line, level],
                outer[line - 1, level], outer[line + 1, level], flat,
            )
            left = own_coarse[line - 1, level] if line else from_left[level, 2 * rows:]
            right = own_coarse[line + 1, level] if line < lines - 1 else from_right[level, 2 * rows:]
            coarse_field = turned(
                coarse_y, shifts_y[2, strip], own_coarse[line, level], left, right, flat
            )
            out[level, :, line * LINE:(line + 1) * LINE] = fine_field - coarse_field


def on_chip(count):
    return [pl.BlockSpec(memory_space=pltpu.VMEM)] * count


def scalars(count):
    return [pl.BlockSpec(memory_space=pltpu.SMEM)] * count


def local(fine_cotangent, coarse_cotangent, upstream_x, upstream_y, fractions):
    levels, slab, width = fine_cotangent.shape
    lines = width // LINE
    reach = lax.axis_size("gx") // 8 * slab
    rows = rounded(slab + 3)
    slabs_fine = -(-(2 * reach + 4) // slab)
    slabs_coarse = -(-(reach + 2) // slab)
    fine = ring_window(fine_cotangent, slabs_fine)
    coarse = ring_window(coarse_cotangent, slabs_coarse)
    like = functools.partial(jax.ShapeDtypeStruct, dtype=fine.dtype)
    sent = like((levels, 2 * rows + slab, LINE))
    own, own_coarse, to_left, to_right = pl.pallas_call(
        functools.partial(sweep_x_kernel, slab, slabs_fine * slab, slabs_coarse * slab),
        out_shape=[
            like((lines, 3, levels, rows, LINE)), like((lines, levels, slab, LINE)), sent, sent,
        ],
        in_specs=scalars(2) + on_chip(2),
        out_specs=on_chip(4),
        scratch_shapes=[
            pltpu.VMEM((lines, *block.shape[:2], LINE), fine.dtype) for block in (fine, coarse)
        ],
    )(upstream_x, fractions, fine, coarse)
    from_left = shifted(to_right, "gy", 1)
    from_right = shifted(to_left, "gy", -1)
    return pl.pallas_call(
        sweep_y_kernel,
        out_shape=like((levels, slab, width)),
        in_specs=scalars(3) + on_chip(4),
        out_specs=on_chip(1)[0],
        scratch_shapes=[pltpu.VMEM((lines + 2, levels, rows, LINE), fine.dtype)],
    )(upstream_x, upstream_y, fractions, own, own_coarse, from_left, from_right)


def solution(mesh):
    placed = (P(None, "gx", "gy"), P(None, "gx", "gy"), P(), P(), P())
    return jax.shard_map(
        local, mesh=mesh, in_specs=placed, out_specs=P(None, "gx", "gy"), check_vma=False
    )
```

time: 67.9 us -> 35.3 us (0.52)
  between operations: 26.6 us -> 0.11 us
  starting transfers between devices: 28.6 us -> 17.3 us
  waiting for transfers between devices: 5.62 us -> 9.79 us
  Pallas kernels: 0 us -> 3.7 us
  other arithmetic: 1.43 us -> 0 us
  local copies, waits for them, and re-layouts: 5.01 us -> 4.1 us
    ppermute x18 -> x12, starting transfers between devices: 28.6 us -> 17.3 us  [shifted(): lax.ppermute(block, axis, [((i - distance) % count, i) for i in range(cou...]
    ppermute x18 -> x12, waiting for transfers between devices: 5.62 us -> 9.79 us  [shifted(): lax.ppermute(block, axis, [((i - distance) % count, i) for i in range(cou...]
    pallas_call x0 -> x2, Pallas kernels: none -> 3.7 us  [the longest x1 1.88 us: local(): pl.pallas_call(sweep_y_kernel, out_shape=like((levels, slab, width)), in_...]
    slice x12 -> x0, local copies, waits for them, and re-layouts: 3.39 us -> none  [the longest x3 1.83 us: sweep_x(): local_shifts[block_index]]
    unnamed x21 -> x26, local copies, waits for them, and re-layouts: 1.46 us -> 4.09 us
    sub x1 -> x0, other arithmetic: 0.75 us -> none  [local(): return fine_field - coarse_field]
  transfers between devices with their start and end apart: 18 -> 12, of which waited for: 4 -> 6; matrix products, arithmetic and copies ran while one was open for 6% -> 6% of each run, Pallas kernels for 0% -> 0%
where the time goes in v1:
time: 35.3 us; the launch traced here: 35 us
  starting transfers between devices  17.3 us (49%)
  waiting for transfers between devices  9.79 us (28%)
  local copies, waits for them, and re-layouts  4.1 us (12%)
  Pallas kernels  3.7 us (10%)
    ppermute x12, starting transfers between devices, shifted(): lax.ppermute(block, axis, [((i - distance) % count, i) for i in range(cou...  17.3 us
    ppermute x12, waiting for transfers between devices, shifted(): lax.ppermute(block, axis, [((i - distance) % count, i) for i in range(cou...  9.79 us
    unnamed x26, local copies, waits for them, and re-layouts  4.09 us
    pallas_call x1, Pallas kernels, local(): pl.pallas_call(sweep_y_kernel, out_shape=like((levels, slab, width)), in_...  1.88 us
    pallas_call x1, Pallas kernels, local(): pl.pallas_call(functools.partial(sweep_x_kernel, slab, slabs_fine * slab,...  1.82 us
  transfers between devices with their start and end apart: 12, of which 6 were waited for; matrix products, arithmetic and copies ran while one was open for 6% of the time, Pallas kernels for 0%

profile of v1, /device:TPU:1, one launch (start us, length us, event | category | flops | bytes accessed | tf_op | source)
XLA Modules:
  0.0 35.0 jit_solution(16374009457864516198)
XLA Ops:
  0.0 3.0 %collective-permute-start = (f32[2,16,256]{2,1,0:T(8,128)}, f32[2,16,256]{2,1,0:T(8,128)S(1)}, u32[]{:S(2)}, u32[]{:S(2)}) collective-permute-start(f32[2,16,256]{2,1,0:T(8,128)} %param.5), channel_id=1, source_target_pairs={{20,0},{24,4},{28,8},{0,12},{4,16},{8,20},{12,24},{16,28},{21,1},{... | collective-permute-start | bytes 98312 | tf_op jit(solution)/shard_map/ppermute | solution.py:21
  3.0 1.3 %collective-permute-start.1 = (f32[2,16,256]{2,1,0:T(8,128)}, f32[2,16,256]{2,1,0:T(8,128)S(1)}, u32[]{:S(2)}, u32[]{:S(2)}) collective-permute-start(f32[2,16,256]{2,1,0:T(8,128)} %param.5), channel_id=1, source_target_pairs={{24,0},{28,4},{0,8},{4,12},{8,16},{12,20},{16,24},{20,28},{25,1},{... | collective-permute-start | bytes 98312 | tf_op jit(solution)/shard_map/ppermute | solution.py:21
  4.3 1.3 %collective-permute-start.2 = (f32[2,16,256]{2,1,0:T(8,128)}, f32[2,16,256]{2,1,0:T(8,128)S(1)}, u32[]{:S(2)}, u32[]{:S(2)}) collective-permute-start(f32[2,16,256]{2,1,0:T(8,128)} %param.5), channel_id=1, source_target_pairs={{28,0},{0,4},{4,8},{8,12},{12,16},{16,20},{20,24},{24,28},{29,1},{... | collective-permute-start | bytes 98312 | tf_op jit(solution)/shard_map/ppermute | solution.py:21
  5.6 2.9 %collective-permute-start.3 = (f32[2,16,256]{2,1,0:T(8,128)}, f32[2,16,256]{2,1,0:T(8,128)S(1)}, u32[]{:S(2)}, u32[]{:S(2)}) collective-permute-start(f32[2,16,256]{2,1,0:T(8,128)} %param.5), channel_id=1, source_target_pairs={{4,0},{8,4},{12,8},{16,12},{20,16},{24,20},{28,24},{0,28},{5,1},{9... | collective-permute-start | bytes 98312 | tf_op jit(solution)/shard_map/ppermute | solution.py:21
  8.5 0.2 collective-permute-start.4
  8.7 1.3 %copy.8.fractions = f32[3,2]{1,0:T(4,128)} copy(f32[3,2]{0,1:T(2,128)} %param.9) | data formatting | bytes 48 | tf_op args[4]
  10.0 0.0 copy-start.5
  10.0 0.0 collective-permute-done
  10.0 0.0 collective-permute-start.5
  10.0 0.0 collective-permute-done.1
  10.1 0.7 %copy-done.5 = f32[2,16,256]{2,1,0:T(8,128)S(1)} copy-done((f32[2,16,256]{2,1,0:T(8,128)S(1)}, f32[2,16,256]{2,1,0:T(8,128)}, u32[]{:S(2)}) %copy-start.5) | copy-done | bytes 32792
  10.8 1.3 %collective-permute-start.6 = (f32[2,16,256]{2,1,0:T(8,128)S(1)}, f32[2,16,256]{2,1,0:T(8,128)S(1)}, u32[]{:S(2)}, u32[]{:S(2)}) collective-permute-start(f32[2,16,256]{2,1,0:T(8,128)S(1)} %copy-done.5), channel_id=1, source_target_pairs={{24,0},{28,4},{0,8},{4,12},{8,16},{12,20},{16,24},{20,28},{25,1},{... | collective-permute-start | bytes 98312 | tf_op jit(solution)/shard_map/ppermute | solution.py:21
  12.1 0.0 copy-start.4
  12.1 0.0 collective-permute-done.2
  12.1 0.7 %collective-permute-start.7 = (f32[2,16,256]{2,1,0:T(8,128)S(1)}, f32[2,16,256]{2,1,0:T(8,128)S(1)}, u32[]{:S(2)}, u32[]{:S(2)}) collective-permute-start(f32[2,16,256]{2,1,0:T(8,128)S(1)} %copy-done.5), channel_id=1, source_target_pairs={{28,0},{0,4},{4,8},{8,12},{12,16},{16,20},{20,24},{24,28},{29,1},{... | collective-permute-start | bytes 98312 | tf_op jit(solution)/shard_map/ppermute | solution.py:21
  12.8 0.0 copy-done.4
  12.8 2.5 %collective-permute-done.6 = f32[2,16,256]{2,1,0:T(8,128)S(1)} collective-permute-done((f32[2,16,256]{2,1,0:T(8,128)S(1)}, f32[2,16,256]{2,1,0:T(8,128)S(1)}, u32[]{:S(2)}, u32[]{:S(2)}) %collective-permute-start.6) | collective-permute-done | bytes 32800 | tf_op jit(solution)/shard_map/ppermute | solution.py:21
  15.3 1.1 %collective-permute-start.8 = (f32[2,16,256]{2,1,0:T(8,128)S(1)}, f32[2,16,256]{2,1,0:T(8,128)S(1)}, u32[]{:S(2)}, u32[]{:S(2)}) collective-permute-start(f32[2,16,256]{2,1,0:T(8,128)S(1)} %copy-done.5), channel_id=1, source_target_pairs={{4,0},{8,4},{12,8},{16,12},{20,16},{24,20},{28,24},{0,28},{5,1},{9... | collective-permute-start | bytes 98312 | tf_op jit(solution)/shard_map/ppermute | solution.py:21
  16.5 1.2 %collective-permute-done.7 = f32[2,16,256]{2,1,0:T(8,128)S(1)} collective-permute-done((f32[2,16,256]{2,1,0:T(8,128)S(1)}, f32[2,16,256]{2,1,0:T(8,128)S(1)}, u32[]{:S(2)}, u32[]{:S(2)}) %collective-permute-start.7) | collective-permute-done | bytes 32800 | tf_op jit(solution)/shard_map/ppermute | solution.py:21
  17.7 0.1 collective-permute-start.9
  17.8 0.0 collective-permute-done.3
  17.8 0.0 collective-permute-done.4
  17.8 0.0 collective-permute-done.5
  17.9 0.0 copy-start
  17.9 0.3 collective-permute-done.8
  18.2 2.5 %collective-permute-done.9 = f32[2,16,256]{2,1,0:T(8,128)S(1)} collective-permute-done((f32[2,16,256]{2,1,0:T(8,128)S(1)}, f32[2,16,256]{2,1,0:T(8,128)S(1)}, u32[]{:S(2)}, u32[]{:S(2)}) %collective-permute-start.9) | collective-permute-done | bytes 32800 | tf_op jit(solution)/shard_map/ppermute | solution.py:21
  20.7 0.0 copy-done
  20.7 0.0 copy-start.1
  20.7 0.7 %copy-done.1 = f32[2,80,256]{2,1,0:T(8,128)} copy-done((f32[2,80,256]{2,1,0:T(8,128)}, f32[2,80,256]{2,1,0:T(8,128)S(1)}, u32[]{:S(2)}) %copy-start.1) | copy-done | bytes 163864
  21.4 1.8 %shard_map.55 = (f32[2,3,2,24,128]{4,3,2,1,0:T(8,128)}, f32[2,2,16,128]{3,2,1,0:T(8,128)}, f32[2,64,128]{2,1,0:T(8,128)}, f32[2,64,128]{2,1,0:T(8,128)}) custom-call(s32[3,8]{1,0:T(4,128)} %shifts_x.1, f32[3,2]{1,0:T(4,128)} %copy.8.fractions, f32[2,112,256]{2,1,0:T(8,128)} %copy-done, f32[2,80,256]{2,1,0:T(8,128)} %copy-done.1), custom_call_target="tpu_custom_call" | custom-call | tf_op jit(solution)/shard_map/pallas_call | solution.py:184
  23.2 0.0 copy-start.6
  23.2 5.4 %collective-permute-start.10 = (f32[2,64,128]{2,1,0:T(8,128)}, f32[2,64,128]{2,1,0:T(8,128)S(1)}, u32[]{:S(2)}, u32[]{:S(2)}) collective-permute-start(f32[2,64,128]{2,1,0:T(8,128)} %get-tuple-element.11), channel_id=1, source_target_pairs={{3,0},{0,1},{1,2},{2,3},{7,4},{4,5},{5,6},{6,7},{11,8},{8,9},{9,10... | collective-permute-start | bytes 196616 | tf_op jit(solution)/shard_map/ppermute | solution.py:21
  28.6 0.0 collective-permute-start.11
  28.6 0.0 copy-done.6
  28.6 0.7 %copy.7.shifts_y = s32[3,1]{1,0:T(4,128)} copy(s32[3,1]{0,1:T(1,128)S(1)} %copy-done.6) | data formatting | bytes 24 | tf_op args[3]
  29.3 1.0 %collective-permute-done.10.from_left = f32[2,64,128]{2,1,0:T(8,128)S(1)} collective-permute-done((f32[2,64,128]{2,1,0:T(8,128)}, f32[2,64,128]{2,1,0:T(8,128)S(1)}, u32[]{:S(2)}, u32[]{:S(2)}) %collective-permute-start.10) | collective-permute-done | bytes 65568 | tf_op jit(solution)/shard_map/ppermute | solution.py:21
  30.3 0.0 copy-start.2
  30.3 2.3 %collective-permute-done.11.from_right = f32[2,64,128]{2,1,0:T(8,128)S(1)} collective-permute-done((f32[2,64,128]{2,1,0:T(8,128)}, f32[2,64,128]{2,1,0:T(8,128)S(1)}, u32[]{:S(2)}, u32[]{:S(2)}) %collective-permute-start.11) | collective-permute-done | bytes 65568 | tf_op jit(solution)/shard_map/ppermute | solution.py:21
  32.5 0.0 copy-start.3
  32.5 0.0 copy-done.2
  32.5 0.6 %copy-done.3 = f32[2,64,128]{2,1,0:T(8,128)} copy-done((f32[2,64,128]{2,1,0:T(8,128)}, f32[2,64,128]{2,1,0:T(8,128)S(1)}, u32[]{:S(2)}) %copy-start.3) | copy-done | bytes 65560
  33.2 1.9 %shard_map.56 = f32[2,16,256]{2,1,0:T(8,128)} custom-call(s32[3,8]{1,0:T(4,128)} %shifts_x.1, s32[3,1]{1,0:T(4,128)} %copy.7.shifts_y, f32[3,2]{1,0:T(4,128)} %copy.8.fractions, f32[2,3,2,24,128]{4,3,2,1,0:T(8,128)} %get-tuple-element.9.own, f32[2,2,16,128]{3,2,1,0:T(8,128)} %get-tuple-element.10.own_coarse, f32[2,64,128]{2,1,0:T(8,128)} %copy-done.2, ...), custom_call_target="tpu_custom_call" | custom-call | tf_op jit(solution)/shard_map/pallas_call | solution.py:197
  (12 shorter events, 0.0 us)
Async XLA Ops:
  0.0 10.0 %collective-permute-start = (f32[2,16,256]{2,1,0:T(8,128)}, f32[2,16,256]{2,1,0:T(8,128)S(1)}, u32[]{:S(2)}, u32[]{:S(2)}) collective-permute-start(f32[2,16,256]{2,1,0:T(8,128)} %param.5), channel_id=1, source_target_pairs={{20,0},{24,4},{28,8},{0,12},{4,16},{8,20},{12,24},{16,28},{21,1},{... | collective-permute-start | bytes 98312 | tf_op jit(solution)/shard_map/ppermute | solution.py:21
  3.0 7.0 %collective-permute-start.1 = (f32[2,16,256]{2,1,0:T(8,128)}, f32[2,16,256]{2,1,0:T(8,128)S(1)}, u32[]{:S(2)}, u32[]{:S(2)}) collective-permute-start(f32[2,16,256]{2,1,0:T(8,128)} %param.5), channel_id=1, source_target_pairs={{24,0},{28,4},{0,8},{4,12},{8,16},{12,20},{16,24},{20,28},{25,1},{... | collective-permute-start | bytes 98312 | tf_op jit(solution)/shard_map/ppermute | solution.py:21
  4.3 7.7 %collective-permute-start.2 = (f32[2,16,256]{2,1,0:T(8,128)}, f32[2,16,256]{2,1,0:T(8,128)S(1)}, u32[]{:S(2)}, u32[]{:S(2)}) collective-permute-start(f32[2,16,256]{2,1,0:T(8,128)} %param.5), channel_id=1, source_target_pairs={{28,0},{0,4},{4,8},{8,12},{12,16},{16,20},{20,24},{24,28},{29,1},{... | collective-permute-start | bytes 98312 | tf_op jit(solution)/shard_map/ppermute | solution.py:21
  5.6 12.2 %collective-permute-start.3 = (f32[2,16,256]{2,1,0:T(8,128)}, f32[2,16,256]{2,1,0:T(8,128)S(1)}, u32[]{:S(2)}, u32[]{:S(2)}) collective-permute-start(f32[2,16,256]{2,1,0:T(8,128)} %param.5), channel_id=1, source_target_pairs={{4,0},{8,4},{12,8},{16,12},{20,16},{24,20},{28,24},{0,28},{5,1},{9... | collective-permute-start | bytes 98312 | tf_op jit(solution)/shard_map/ppermute | solution.py:21
  8.5 9.3 %collective-permute-start.4 = (f32[2,16,256]{2,1,0:T(8,128)}, f32[2,16,256]{2,1,0:T(8,128)S(1)}, u32[]{:S(2)}, u32[]{:S(2)}) collective-permute-start(f32[2,16,256]{2,1,0:T(8,128)} %param.5), channel_id=1, source_target_pairs={{8,0},{12,4},{16,8},{20,12},{24,16},{28,20},{0,24},{4,28},{9,1},{1... | collective-permute-start | bytes 98312 | tf_op jit(solution)/shard_map/ppermute | solution.py:21
  10.0 0.8 %copy-start.5 = (f32[2,16,256]{2,1,0:T(8,128)S(1)}, f32[2,16,256]{2,1,0:T(8,128)}, u32[]{:S(2)}) copy-start(f32[2,16,256]{2,1,0:T(8,128)} %param.6) | copy-start | bytes 98308
  10.0 7.8 %collective-permute-start.5 = (f32[2,16,256]{2,1,0:T(8,128)}, f32[2,16,256]{2,1,0:T(8,128)S(1)}, u32[]{:S(2)}, u32[]{:S(2)}) collective-permute-start(f32[2,16,256]{2,1,0:T(8,128)} %param.5), channel_id=1, source_target_pairs={{12,0},{16,4},{20,8},{24,12},{28,16},{0,20},{4,24},{8,28},{13,1},{... | collective-permute-start | bytes 98312 | tf_op jit(solution)/shard_map/ppermute | solution.py:21
  10.8 4.6 %collective-permute-start.6 = (f32[2,16,256]{2,1,0:T(8,128)S(1)}, f32[2,16,256]{2,1,0:T(8,128)S(1)}, u32[]{:S(2)}, u32[]{:S(2)}) collective-permute-start(f32[2,16,256]{2,1,0:T(8,128)S(1)} %copy-done.5), channel_id=1, source_target_pairs={{24,0},{28,4},{0,8},{4,12},{8,16},{12,20},{16,24},{20,28},{25,1},{... | collective-permute-start | bytes 98312 | tf_op jit(solution)/shard_map/ppermute | solution.py:21
  12.1 0.8 %copy-start.4 = (f32[2,16,256]{2,1,0:T(8,128)S(1)}, f32[2,16,256]{2,1,0:T(8,128)}, u32[]{:S(2)}) copy-start(f32[2,16,256]{2,1,0:T(8,128)} %param.5) | copy-start | bytes 98308
  12.1 5.6 %collective-permute-start.7 = (f32[2,16,256]{2,1,0:T(8,128)S(1)}, f32[2,16,256]{2,1,0:T(8,128)S(1)}, u32[]{:S(2)}, u32[]{:S(2)}) collective-permute-start(f32[2,16,256]{2,1,0:T(8,128)S(1)} %copy-done.5), channel_id=1, source_target_pairs={{28,0},{0,4},{4,8},{8,12},{12,16},{16,20},{20,24},{24,28},{29,1},{... | collective-permute-start | bytes 98312 | tf_op jit(solution)/shard_map/ppermute | solution.py:21
  15.3 2.8 %collective-permute-start.8 = (f32[2,16,256]{2,1,0:T(8,128)S(1)}, f32[2,16,256]{2,1,0:T(8,128)S(1)}, u32[]{:S(2)}, u32[]{:S(2)}) collective-permute-start(f32[2,16,256]{2,1,0:T(8,128)S(1)} %copy-done.5), channel_id=1, source_target_pairs={{4,0},{8,4},{12,8},{16,12},{20,16},{24,20},{28,24},{0,28},{5,1},{9... | collective-permute-start | bytes 98312 | tf_op jit(solution)/shard_map/ppermute | solution.py:21
  17.7 3.0 %collective-permute-start.9 = (f32[2,16,256]{2,1,0:T(8,128)S(1)}, f32[2,16,256]{2,1,0:T(8,128)S(1)}, u32[]{:S(2)}, u32[]{:S(2)}) collective-permute-start(f32[2,16,256]{2,1,0:T(8,128)S(1)} %copy-done.5), channel_id=1, source_target_pairs={{8,0},{12,4},{16,8},{20,12},{24,16},{28,20},{0,24},{4,28},{9,1},{1... | collective-permute-start | bytes 98312 | tf_op jit(solution)/shard_map/ppermute | solution.py:21
  17.9 2.9 %copy-start = (f32[2,112,256]{2,1,0:T(8,128)}, f32[2,112,256]{2,1,0:T(8,128)S(1)}, u32[]{:S(2)}) copy-start(f32[2,112,256]{2,1,0:T(8,128)S(1)} %constant_dynamic-update-slice_fusion.fine) | copy-start | bytes 688132
  20.7 0.7 %copy-start.1 = (f32[2,80,256]{2,1,0:T(8,128)}, f32[2,80,256]{2,1,0:T(8,128)S(1)}, u32[]{:S(2)}) copy-start(f32[2,80,256]{2,1,0:T(8,128)S(1)} %constant_dynamic-update-slice_fusion.7.coarse) | copy-start | bytes 491524
  23.2 5.4 %copy-start.6 = (s32[3,1]{0,1:T(1,128)S(1)}, s32[3,1]{0,1:T(1,128)}, u32[]{:S(2)}) copy-start(s32[3,1]{0,1:T(1,128)} %param.8) | copy-start | bytes 40
  23.2 7.1 %collective-permute-start.10 = (f32[2,64,128]{2,1,0:T(8,128)}, f32[2,64,128]{2,1,0:T(8,128)S(1)}, u32[]{:S(2)}, u32[]{:S(2)}) collective-permute-start(f32[2,64,128]{2,1,0:T(8,128)} %get-tuple-element.11), channel_id=1, source_target_pairs={{3,0},{0,1},{1,2},{2,3},{7,4},{4,5},{5,6},{6,7},{11,8},{8,9},{9,10... | collective-permute-start | bytes 196616 | tf_op jit(solution)/shard_map/ppermute | solution.py:21
  28.6 3.9 %collective-permute-start.11 = (f32[2,64,128]{2,1,0:T(8,128)}, f32[2,64,128]{2,1,0:T(8,128)S(1)}, u32[]{:S(2)}, u32[]{:S(2)}) collective-permute-start(f32[2,64,128]{2,1,0:T(8,128)} %get-tuple-element.12), channel_id=1, source_target_pairs={{1,0},{2,1},{3,2},{0,3},{5,4},{6,5},{7,6},{4,7},{9,8},{10,9},{11,1... | collective-permute-start | bytes 196616 | tf_op jit(solution)/shard_map/ppermute | solution.py:21
  30.3 2.3 %copy-start.2 = (f32[2,64,128]{2,1,0:T(8,128)}, f32[2,64,128]{2,1,0:T(8,128)S(1)}, u32[]{:S(2)}) copy-start(f32[2,64,128]{2,1,0:T(8,128)S(1)} %collective-permute-done.10.from_left) | copy-start | bytes 196612
  32.5 0.6 %copy-start.3 = (f32[2,64,128]{2,1,0:T(8,128)}, f32[2,64,128]{2,1,0:T(8,128)S(1)}, u32[]{:S(2)}) copy-start(f32[2,64,128]{2,1,0:T(8,128)S(1)} %collective-permute-done.11.from_right) | copy-start | bytes 196612

commit v2 on v1

v2 whole, which is shorter than its diff:
```python
import functools

import jax
import jax.numpy as jnp
from jax import lax
from jax.experimental import pallas as pl
from jax.experimental.pallas import tpu as pltpu
from jax.sharding import PartitionSpec as P

LINE = 128
MAXDY = 32
EDGE = 8


def rounded(rows):
    return -(-rows // EDGE) * EDGE


def exchanged(block, axis, partner):
    return lax.ppermute(block, axis, [(i, partner(i)) for i in range(lax.axis_size(axis))])


def shifted(block, axis, distance):
    count = lax.axis_size(axis)
    return exchanged(block, axis, lambda i: (i + distance) % count)


def ring_window(block, slabs):
    lower = [shifted(block, "gx", distance) for distance in range(slabs, 0, -1)]
    upper = [shifted(block, "gx", -distance) for distance in range(1, slabs + 1)]
    return jnp.concatenate(lower + [block] + upper, axis=1)


def cubic_weights(fraction):
    position = 1.0 - fraction
    return (
        -position * (position - 1.0) * (position - 2.0) * (1.0 / 6.0),
        (position + 1.0) * (position - 1.0) * (position - 2.0) * 0.5,
        -(position + 1.0) * position * (position - 2.0) * 0.5,
        (position + 1.0) * position * (position - 1.0) * (1.0 / 6.0),
    )


def weighted(weights, term):
    summed = weights[0] * term(0)
    for tap in range(1, 4):
        summed = summed + weights[tap] * term(tap)
    return summed


def aligned(start, size):
    return pl.ds(pl.multiple_of(start, EDGE), size)


def column_side():
    return lax.axis_index("gx") % 2


def layer_side():
    return lax.axis_index("gx") // 2 % 2


def relay_kernel(near, far, opposite, relay):
    both = near.shape[1]
    slab = both // 2
    column = column_side()
    start = (1 - column) * (slab - EDGE)
    swapped = (column + layer_side()) % 2

    def send(whole, partial):
        relay[:, :both] = whole[...]
        relay[:, both:both + EDGE] = partial[:, aligned(start, EDGE)]

    @pl.when(swapped == 0)
    def _():
        send(near, far)

    @pl.when(swapped == 1)
    def _():
        send(far, near)

    relay[:, both + EDGE:] = opposite[...]


def fill_whole(fine, coarse, fine_lines, coarse_lines):
    for line in range(fine_lines.shape[0]):
        lanes = slice(line * LINE, (line + 1) * LINE)
        fine_lines[line] = fine[:, :, lanes]
        coarse_lines[line] = coarse[:, :, lanes]


def fill_pieces(own, beside, near, far, relay, fine_lines, coarse_lines):
    both = own.shape[1]
    slab = both // 2
    column = 1 - 2 * column_side()
    layer = 1 - 2 * layer_side()
    fine_center = (fine_lines.shape[2] - slab) // 2
    coarse_center = (coarse_lines.shape[2] - slab) // 2
    below = fine_center - 2 * slab - EDGE
    above = fine_center + 3 * slab
    for line in range(fine_lines.shape[0]):
        lanes = slice(line * LINE, (line + 1) * LINE)
        for piece, slabs in (
            (own, 0), (beside, column), (near, 2 * layer), (far, -2 * layer), (relay, -column),
        ):
            fine_lines[line, :, aligned(fine_center + slabs * slab, slab)] = piece[:, :slab, lanes]
            coarse_lines[line, :, aligned(coarse_center + slabs * slab, slab)] = (
                piece[:, slab:both, lanes]
            )
        for start, up in ((both, column), (both + EDGE, -column)):
            row = below + (above - below) // 2 * (1 + up)
            fine_lines[line, :, aligned(row, EDGE)] = relay[:, start:start + EDGE, lanes]


def sweep_x_kernel(fill, shifts, fractions, *refs):
    *gathered, own, own_coarse, to_near, to_far, fine_lines, coarse_lines = refs
    lines, levels, _, _ = fine_lines.shape
    rows = own.shape[3]
    slab = own_coarse.shape[2]
    total = shifts.shape[1]
    first = lax.axis_index("gy") * lines
    fine_center = (fine_lines.shape[2] - slab) // 2
    coarse_center = (coarse_lines.shape[2] - slab) // 2
    fine_weights = cubic_weights(fractions[0, 1])
    coarse_weights = cubic_weights(fractions[0, 2])
    fill(*gathered, fine_lines, coarse_lines)
    for line in range(lines):
        inner = shifts[1, first + line]
        for slot in range(3):
            region = lax.rem(first + line + slot - 1 + total, total)
            start = fine_center - 1 + inner + shifts[0, region]
            for level in range(levels):
                own[line, slot, level] = weighted(
                    fine_weights,
                    lambda tap: fine_lines[line, level, pl.ds(start + 2 - tap, rows)],
                )
        start = coarse_center + shifts[2, first + line]
        for level in range(levels):
            own_coarse[line, level] = weighted(
                coarse_weights,
                lambda tap: coarse_lines[line, level, pl.ds(start + 2 - tap, slab)],
            )
    near_right = lax.axis_index("gy") % 2 == 0
    for level in range(levels):
        leftward = own[0, 0, level], own[0, 1, level], own_coarse[0, level]
        rightward = own[lines - 1, 1, level], own[lines - 1, 2, level], own_coarse[lines - 1, level]
        for start, left, right in zip((0, rows, 2 * rows), leftward, rightward):
            part = slice(start, start + left.shape[0])
            to_near[level, part] = jnp.where(near_right, right, left)
            to_far[level, part] = jnp.where(near_right, left, right)


def turned(weights, offset, current, left, right, lane):
    beside = jnp.where(lane < LINE // 2, right, left)

    def term(tap):
        distance = offset + 2 - tap
        outside = (lane < distance) | (lane >= LINE + distance)
        mixed = jnp.where(outside, beside, current)
        return pltpu.roll(mixed, lax.rem(LINE - distance, LINE), 1)

    return weighted(weights, term)


def sweep_y_kernel(shifts_x, shifts_y, fractions, own, own_coarse, from_near, from_far, out, held):
    lines, _, levels, rows, _ = own.shape
    slab = own_coarse.shape[2]
    total = shifts_x.shape[1]
    strips = shifts_y.shape[0]
    first = lax.axis_index("gy") * lines
    base = lax.axis_index("gx") * slab
    extent = lax.axis_size("gx") * slab
    outer_x = cubic_weights(fractions[0, 0])
    outer_y = cubic_weights(fractions[1, 0])
    inner_y = cubic_weights(fractions[1, 1])
    coarse_y = cubic_weights(fractions[1, 2])
    tall = lax.broadcasted_iota(jnp.int32, (rows, LINE), 1)
    flat = lax.broadcasted_iota(jnp.int32, (slab, LINE), 1)
    strip = lax.div(base, LINE)
    near_right = lax.axis_index("gy") % 2 == 0

    def from_left(level, start, size):
        part = slice(start, start + size)
        return jnp.where(near_right, from_far[level, part], from_near[level, part])

    def from_right(level, start, size):
        part = slice(start, start + size)
        return jnp.where(near_right, from_near[level, part], from_far[level, part])

    def pieces(region, level):
        if region < 0:
            current = from_left(level, 0, rows)
            return current, current, own[0, 0, level]
        if region == lines:
            current = from_right(level, rows, rows)
            return current, own[lines - 1, 2, level], current
        left = own[region - 1, 2, level] if region else from_left(level, rows, rows)
        right = own[region + 1, 0, level] if region < lines - 1 else from_right(level, 0, rows)
        return own[region, 1, level], left, right

    outer = {}
    for region in range(-1, lines + 1):
        if strips > 1:
            shift = shifts_x[0, lax.rem(first + region + total, total)]
            start = lax.rem(base + shift - 1 + extent, extent)
            here = lax.div(start, LINE)
            after = lax.rem(here + 1, strips)
            row = lax.broadcasted_iota(jnp.int32, (rows, LINE), 0)
            beyond = row >= LINE - lax.rem(start, LINE)
        for level in range(levels):
            current, left, right = pieces(region, level)
            if strips > 1:
                swept = jnp.where(
                    beyond,
                    turned(inner_y, shifts_y[after, 1], current, left, right, tall),
                    turned(inner_y, shifts_y[here, 1], current, left, right, tall),
                )
            else:
                swept = turned(inner_y, shifts_y[0, 1], current, left, right, tall)
            held[region + 1, level] = swept
            outer[region, level] = weighted(
                outer_x, lambda tap: held[region + 1, level, 3 - tap:3 - tap + slab]
            )
    for line in range(lines):
        for level in range(levels):
            fine_field = turned(
                outer_y, shifts_y[strip, 0], outer[line, level],
                outer[line - 1, level], outer[line + 1, level], flat,
            )
            left = own_coarse[line - 1, level] if line else from_left(level, 2 * rows, slab)
            right = (
                own_coarse[line + 1, level] if line < lines - 1
                else from_right(level, 2 * rows, slab)
            )
            coarse_field = turned(
                coarse_y, shifts_y[strip, 2], own_coarse[line, level], left, right, flat
            )
            out[level, :, line * LINE:(line + 1) * LINE] = fine_field - coarse_field


def on_chip(count):
    return [pl.BlockSpec(memory_space=pltpu.VMEM)] * count


def scalars(count):
    return [pl.BlockSpec(memory_space=pltpu.SMEM)] * count


def local(fine_cotangent, coarse_cotangent, upstream_x, upstream_y, fractions):
    levels, slab, width = fine_cotangent.shape
    lines = width // LINE
    count_x = lax.axis_size("gx")
    count_y = lax.axis_size("gy")
    reach = count_x // 8 * slab
    rows = rounded(slab + 3)
    slabs_fine = -(-(2 * reach + 4) // slab)
    slabs_coarse = -(-(reach + 2) // slab)
    like = functools.partial(jax.ShapeDtypeStruct, dtype=fine_cotangent.dtype)
    windows = [
        pltpu.VMEM((lines, levels, (2 * slabs + 1) * slab, LINE), fine_cotangent.dtype)
        for slabs in (slabs_fine, slabs_coarse)
    ]
    limit = (4 << 20) + 12 * levels * (slabs_fine + slabs_coarse + 1) * slab * width * 4
    params = pltpu.CompilerParams(vmem_limit_bytes=limit)
    if count_x == 8 and slab == 2 * EDGE:
        packed = jnp.concatenate([fine_cotangent, coarse_cotangent], axis=1)
        packed = lax.optimization_barrier(packed)
        edge = lax.dynamic_slice_in_dim(packed, column_side() * (slab - EDGE), EDGE, 1)
        beside = exchanged(packed, "gx", lambda i: i ^ 1)
        near = exchanged(packed, "gx", lambda i: i ^ 2)
        opposite = exchanged(edge, "gx", lambda i: i ^ 4)
        far = exchanged(packed, "gx", lambda i: i ^ 6)
        beside, near, opposite, far = lax.optimization_barrier((beside, near, opposite, far))
        relay = pl.pallas_call(
            relay_kernel,
            out_shape=like((levels, 2 * slab + 2 * EDGE, width)),
            in_specs=on_chip(3),
            out_specs=on_chip(1)[0],
            compiler_params=params,
        )(near, far, opposite)
        relay = exchanged(relay, "gx", lambda i: i ^ 1)
        fill = fill_pieces
        gathered = packed, beside, near, far, relay
    else:
        fill = fill_whole
        gathered = ring_window(fine_cotangent, slabs_fine), ring_window(coarse_cotangent, slabs_coarse)
    sent = like((levels, 2 * rows + slab, LINE))
    own, own_coarse, to_near, to_far = pl.pallas_call(
        functools.partial(sweep_x_kernel, fill),
        out_shape=[
            like((lines, 3, levels, rows, LINE)), like((lines, levels, slab, LINE)), sent, sent,
        ],
        in_specs=scalars(2) + on_chip(len(gathered)),
        out_specs=on_chip(4),
        scratch_shapes=windows,
        compiler_params=params,
    )(upstream_x, fractions.T, *gathered)
    from_near = exchanged(to_near, "gy", lambda j: j ^ 1)
    from_far = exchanged(to_far, "gy", lambda j: (j - 1 + 2 * (j % 2)) % count_y)
    return pl.pallas_call(
        sweep_y_kernel,
        out_shape=like((levels, slab, width)),
        in_specs=scalars(3) + on_chip(4),
        out_specs=on_chip(1)[0],
        scratch_shapes=[pltpu.VMEM((lines + 2, levels, rows, LINE), fine_cotangent.dtype)],
        compiler_params=params,
    )(upstream_x, upstream_y.T, fractions.T, own, own_coarse, from_near, from_far)


def solution(mesh):
    placed = (P(None, "gx", "gy"), P(None, "gx", "gy"), P(), P(), P())
    return jax.shard_map(
        local, mesh=mesh, in_specs=placed, out_specs=P(None, "gx", "gy"), check_vma=False
    )
```

time: 35.3 us -> 23.7 us (0.67)
  starting transfers between devices: 17.3 us -> 10.8 us
  local copies, waits for them, and re-layouts: 4.1 us -> 0.67 us
  Pallas kernels: 3.7 us -> 2.23 us
  waiting for transfers between devices: 9.79 us -> 8.93 us
  other arithmetic: 0 us -> 0.78 us
    ppermute x12 -> x7, starting transfers between devices: 17.3 us -> 10.8 us  [exchanged(): lax.ppermute(block, axis, [(i, partner(i)) for i in range(lax.axis_size(a...]
    unnamed x26 -> x6, local copies, waits for them, and re-layouts: 4.09 us -> 0.67 us
    pallas_call x1 -> x2, Pallas kernels: 1.82 us -> 0.72 us  [the longest x1 0.68 us: local(): pl.pallas_call(functools.partial(sweep_x_kernel, fill), out_shape=[like((...]
    ppermute x12 -> x7, waiting for transfers between devices: 9.79 us -> 8.93 us  [exchanged(): lax.ppermute(block, axis, [(i, partner(i)) for i in range(lax.axis_size(a...]
    concatenate x0 -> x1, other arithmetic: none -> 0.78 us  [local(): packed = jnp.concatenate([fine_cotangent, coarse_cotangent], axis=1)]
    pallas_call x1, Pallas kernels: 1.88 us -> 1.5 us  [local(): pl.pallas_call(sweep_y_kernel, out_shape=like((levels, slab, width)), in_...]
  transfers between devices with their start and end apart: 12 -> 7, of which waited for: 6 -> 3; matrix products, arithmetic and copies ran while one was open for 6% -> 0% of each run, Pallas kernels for 0% -> 0%
where the time goes in v2:
time: 23.7 us; the launch traced here: 23.5 us
  starting transfers between devices  10.8 us (46%)
  waiting for transfers between devices  8.93 us (38%)
  Pallas kernels  2.23 us (9%)
  other arithmetic  0.78 us (3%)
  local copies, waits for them, and re-layouts  0.67 us (3%)
    ppermute x7, starting transfers between devices, exchanged(): lax.ppermute(block, axis, [(i, partner(i)) for i in range(lax.axis_size(a...  10.8 us
    ppermute x7, waiting for transfers between devices, exchanged(): lax.ppermute(block, axis, [(i, partner(i)) for i in range(lax.axis_size(a...  8.93 us
    pallas_call x1, Pallas kernels, local(): pl.pallas_call(sweep_y_kernel, out_shape=like((levels, slab, width)), in_...  1.5 us
    concatenate x1, other arithmetic, local(): packed = jnp.concatenate([fine_cotangent, coarse_cotangent], axis=1)  0.78 us
    pallas_call x1, Pallas kernels, local(): pl.pallas_call(functools.partial(sweep_x_kernel, fill), out_shape=[like((...  0.68 us
    unnamed x6, local copies, waits for them, and re-layouts  0.67 us
  transfers between devices with their start and end apart: 7, of which 3 were waited for; matrix products, arithmetic and copies ran while one was open for 0% of the time, Pallas kernels for 0%

profile of v2, /device:TPU:1, one launch (start us, length us, event | category | flops | bytes accessed | tf_op | source)
XLA Modules:
  0.0 23.5 jit_solution(6488190479981461495)
XLA Ops:
  0.0 0.8 %pad_maximum_fusion.refs_0_ = f32[2,32,256]{2,1,0:T(8,128)S(1)} fusion(f32[2,16,256]{2,1,0:T(8,128)} %param.6, f32[2,16,256]{2,1,0:T(8,128)} %param.5), kind=kLoop, calls=%fused_computation | loop fusion | flops 16384 | bytes 131072 | tf_op jit(solution)/shard_map/concatenate | solution.py:266
  0.8 4.1 %collective-permute-start.3 = (f32[2,32,256]{2,1,0:T(8,128)S(1)}, f32[2,32,256]{2,1,0:T(8,128)S(1)}, u32[]{:S(2)}, u32[]{:S(2)}) collective-permute-start(f32[2,32,256]{2,1,0:T(8,128)S(1)} %pad_maximum_fusion.refs_0_), channel_id=1, source_target_pairs={{0,24},{4,28},{8,16},{12,20},{16,8},{20,12},{24,0},{28,4},{1,25},{... | collective-permute-start | bytes 196616 | tf_op jit(solution)/shard_map/ppermute | solution.py:20
  4.9 0.0 collective-permute-start.1
  4.9 1.2 %collective-permute-start = (f32[2,32,256]{2,1,0:T(8,128)S(1)}, f32[2,32,256]{2,1,0:T(8,128)S(1)}, u32[]{:S(2)}, u32[]{:S(2)}) collective-permute-start(f32[2,32,256]{2,1,0:T(8,128)S(1)} %pad_maximum_fusion.refs_0_), channel_id=1, source_target_pairs={{0,4},{4,0},{8,12},{12,8},{16,20},{20,16},{24,28},{28,24},{1,5},{5... | collective-permute-start | bytes 196616 | tf_op jit(solution)/shard_map/ppermute | solution.py:20
  6.1 0.4 %collective-permute-start.2 = (f32[2,8,256]{2,1,0:T(8,128)S(1)}, f32[2,8,256]{2,1,0:T(8,128)S(1)}, u32[]{:S(2)}, u32[]{:S(2)}) collective-permute-start(f32[2,8,256]{2,1,0:T(8,128)S(1)} %constant_dynamic-slice_fusion), channel_id=1, source_target_pairs={{0,16},{4,20},{8,24},{12,28},{16,0},{20,4},{24,8},{28,12},{1,17},{... | collective-permute-start | bytes 49160 | tf_op jit(solution)/shard_map/ppermute | solution.py:20
  6.5 3.1 %collective-permute-done.2.opposite = f32[2,8,256]{2,1,0:T(8,128)S(1)} collective-permute-done((f32[2,8,256]{2,1,0:T(8,128)S(1)}, f32[2,8,256]{2,1,0:T(8,128)S(1)}, u32[]{:S(2)}, u32[]{:S(2)}) %collective-permute-start.2) | collective-permute-done | bytes 16416 | tf_op jit(solution)/shard_map/ppermute | solution.py:20
  9.6 0.0 collective-permute-done.3.far.refs_3_
  9.6 0.0 collective-permute-done.1.near.refs_2_
  9.6 0.0 collective-permute-done.refs_1_
  9.6 0.0 copy-start
  9.7 0.0 copy-start.1
  9.7 0.3 %collective-permute-start.4 = (f32[2,48,256]{2,1,0:T(8,128)S(1)}, f32[2,48,256]{2,1,0:T(8,128)S(1)}, u32[]{:S(2)}, u32[]{:S(2)}) collective-permute-start(f32[2,48,256]{2,1,0:T(8,128)S(1)} %shard_map.55), channel_id=1, source_target_pairs={{0,4},{4,0},{8,12},{12,8},{16,20},{20,16},{24,28},{28,24},{1,5},{5... | collective-permute-start | bytes 294920 | tf_op jit(solution)/shard_map/ppermute | solution.py:20
  10.0 3.2 %collective-permute-done.4.refs_4_ = f32[2,48,256]{2,1,0:T(8,128)S(1)} collective-permute-done((f32[2,48,256]{2,1,0:T(8,128)S(1)}, f32[2,48,256]{2,1,0:T(8,128)S(1)}, u32[]{:S(2)}, u32[]{:S(2)}) %collective-permute-start.4) | collective-permute-done | bytes 98336 | tf_op jit(solution)/shard_map/ppermute | solution.py:20
  13.2 0.0 copy-done
  13.2 0.0 copy-done.1
  13.3 0.7 %shard_map.56 = (f32[2,3,2,24,128]{4,3,2,1,0:T(8,128)S(1)}, f32[2,2,16,128]{3,2,1,0:T(8,128)S(1)}, f32[2,64,128]{2,1,0:T(8,128)S(1)}, f32[2,64,128]{2,1,0:T(8,128)S(1)}) custom-call(s32[3,8]{1,0:T(4,128)S(1)} %copy-done, f32[2,3]{1,0:T(2,128)S(1)} %bitcast.2, f32[2,32,256]{2,1,0:T(8,128)S(1)} %pad_maximum_fusion.refs_0_, ...), custom_call_target="tpu_custom_call" | custom-call | tf_op jit(solution)/shard_map/pallas_call | solution.py:288
  13.9 3.6 %collective-permute-start.5 = (f32[2,64,128]{2,1,0:T(8,128)S(1)}, f32[2,64,128]{2,1,0:T(8,128)S(1)}, u32[]{:S(2)}, u32[]{:S(2)}) collective-permute-start(f32[2,64,128]{2,1,0:T(8,128)S(1)} %get-tuple-element.19), channel_id=1, source_target_pairs={{0,1},{1,0},{2,3},{3,2},{4,5},{5,4},{6,7},{7,6},{8,9},{9,8},{10,11... | collective-permute-start | bytes 196616 | tf_op jit(solution)/shard_map/ppermute | solution.py:20
  17.5 1.2 %collective-permute-start.6 = (f32[2,64,128]{2,1,0:T(8,128)S(1)}, f32[2,64,128]{2,1,0:T(8,128)S(1)}, u32[]{:S(2)}, u32[]{:S(2)}) collective-permute-start(f32[2,64,128]{2,1,0:T(8,128)S(1)} %get-tuple-element.20), channel_id=1, source_target_pairs={{0,3},{1,2},{2,1},{3,0},{4,7},{5,6},{6,5},{7,4},{8,11},{9,10},{10,... | collective-permute-start | bytes 196616 | tf_op jit(solution)/shard_map/ppermute | solution.py:20
  18.7 0.0 collective-permute-done.5.from_near
  18.7 2.6 %collective-permute-done.6.from_far = f32[2,64,128]{2,1,0:T(8,128)S(1)} collective-permute-done((f32[2,64,128]{2,1,0:T(8,128)S(1)}, f32[2,64,128]{2,1,0:T(8,128)S(1)}, u32[]{:S(2)}, u32[]{:S(2)}) %collective-permute-start.6) | collective-permute-done | bytes 65568 | tf_op jit(solution)/shard_map/ppermute | solution.py:20
  21.3 0.0 copy-start.2
  21.3 0.7 %copy-done.2 = s32[3,1]{0,1:T(1,128)S(1)} copy-done((s32[3,1]{0,1:T(1,128)S(1)}, s32[3,1]{0,1:T(1,128)}, u32[]{:S(2)}) %copy-start.2) | copy-done | bytes 36
  22.0 1.5 %shard_map.57 = f32[2,16,256]{2,1,0:T(8,128)} custom-call(s32[3,8]{1,0:T(4,128)S(1)} %copy-done, s32[1,3]{1,0:T(1,128)S(1)} %bitcast.4, f32[2,3]{1,0:T(2,128)S(1)} %bitcast.3, f32[2,3,2,24,128]{4,3,2,1,0:T(8,128)S(1)} %get-tuple-element.17.own, f32[2,2,16,128]{3,2,1,0:T(8,128)S(1)} %get-tuple-element.18.own_coarse, ...), custom_call_target="tpu_custom_call" | custom-call | tf_op jit(solution)/shard_map/pallas_call | solution.py:300
  (2 shorter events, 0.0 us)
Async XLA Ops:
  0.8 8.8 %collective-permute-start.3 = (f32[2,32,256]{2,1,0:T(8,128)S(1)}, f32[2,32,256]{2,1,0:T(8,128)S(1)}, u32[]{:S(2)}, u32[]{:S(2)}) collective-permute-start(f32[2,32,256]{2,1,0:T(8,128)S(1)} %pad_maximum_fusion.refs_0_), channel_id=1, source_target_pairs={{0,24},{4,28},{8,16},{12,20},{16,8},{20,12},{24,0},{28,4},{1,25},{... | collective-permute-start | bytes 196616 | tf_op jit(solution)/shard_map/ppermute | solution.py:20
  4.9 4.7 %collective-permute-start.1 = (f32[2,32,256]{2,1,0:T(8,128)S(1)}, f32[2,32,256]{2,1,0:T(8,128)S(1)}, u32[]{:S(2)}, u32[]{:S(2)}) collective-permute-start(f32[2,32,256]{2,1,0:T(8,128)S(1)} %pad_maximum_fusion.refs_0_), channel_id=1, source_target_pairs={{0,8},{4,12},{8,0},{12,4},{16,24},{20,28},{24,16},{28,20},{1,9},{5... | collective-permute-start | bytes 196616 | tf_op jit(solution)/shard_map/ppermute | solution.py:20
  4.9 4.7 %collective-permute-start = (f32[2,32,256]{2,1,0:T(8,128)S(1)}, f32[2,32,256]{2,1,0:T(8,128)S(1)}, u32[]{:S(2)}, u32[]{:S(2)}) collective-permute-start(f32[2,32,256]{2,1,0:T(8,128)S(1)} %pad_maximum_fusion.refs_0_), channel_id=1, source_target_pairs={{0,4},{4,0},{8,12},{12,8},{16,20},{20,16},{24,28},{28,24},{1,5},{5... | collective-permute-start | bytes 196616 | tf_op jit(solution)/shard_map/ppermute | solution.py:20
  6.1 3.5 %collective-permute-start.2 = (f32[2,8,256]{2,1,0:T(8,128)S(1)}, f32[2,8,256]{2,1,0:T(8,128)S(1)}, u32[]{:S(2)}, u32[]{:S(2)}) collective-permute-start(f32[2,8,256]{2,1,0:T(8,128)S(1)} %constant_dynamic-slice_fusion), channel_id=1, source_target_pairs={{0,16},{4,20},{8,24},{12,28},{16,0},{20,4},{24,8},{28,12},{1,17},{... | collective-permute-start | bytes 49160 | tf_op jit(solution)/shard_map/ppermute | solution.py:20
  9.6 3.6 %copy-start = (s32[3,8]{1,0:T(4,128)S(1)}, s32[3,8]{1,0:T(4,128)}, u32[]{:S(2)}) copy-start(s32[3,8]{1,0:T(4,128)} %shifts_x.1) | copy-start | bytes 292
  9.7 3.5 %copy-start.1 = (f32[3,2]{0,1:T(2,128)S(1)}, f32[3,2]{0,1:T(2,128)}, u32[]{:S(2)}) copy-start(f32[3,2]{0,1:T(2,128)} %param.9) | copy-start | bytes 76
  9.7 3.5 %collective-permute-start.4 = (f32[2,48,256]{2,1,0:T(8,128)S(1)}, f32[2,48,256]{2,1,0:T(8,128)S(1)}, u32[]{:S(2)}, u32[]{:S(2)}) collective-permute-start(f32[2,48,256]{2,1,0:T(8,128)S(1)} %shard_map.55), channel_id=1, source_target_pairs={{0,4},{4,0},{8,12},{12,8},{16,20},{20,16},{24,28},{28,24},{1,5},{5... | collective-permute-start | bytes 294920 | tf_op jit(solution)/shard_map/ppermute | solution.py:20
  13.9 4.8 %collective-permute-start.5 = (f32[2,64,128]{2,1,0:T(8,128)S(1)}, f32[2,64,128]{2,1,0:T(8,128)S(1)}, u32[]{:S(2)}, u32[]{:S(2)}) collective-permute-start(f32[2,64,128]{2,1,0:T(8,128)S(1)} %get-tuple-element.19), channel_id=1, source_target_pairs={{0,1},{1,0},{2,3},{3,2},{4,5},{5,4},{6,7},{7,6},{8,9},{9,8},{10,11... | collective-permute-start | bytes 196616 | tf_op jit(solution)/shard_map/ppermute | solution.py:20
  17.5 3.8 %collective-permute-start.6 = (f32[2,64,128]{2,1,0:T(8,128)S(1)}, f32[2,64,128]{2,1,0:T(8,128)S(1)}, u32[]{:S(2)}, u32[]{:S(2)}) collective-permute-start(f32[2,64,128]{2,1,0:T(8,128)S(1)} %get-tuple-element.20), channel_id=1, source_target_pairs={{0,3},{1,2},{2,1},{3,0},{4,7},{5,6},{6,5},{7,4},{8,11},{9,10},{10,... | collective-permute-start | bytes 196616 | tf_op jit(solution)/shard_map/ppermute | solution.py:20
  21.3 0.7 %copy-start.2 = (s32[3,1]{0,1:T(1,128)S(1)}, s32[3,1]{0,1:T(1,128)}, u32[]{:S(2)}) copy-start(s32[3,1]{0,1:T(1,128)} %param.8) | copy-start | bytes 40

commit v3 on v2

--- a/solution.py
+++ b/solution.py
@@ -7,9 +7,11 @@
 from jax.experimental.pallas import tpu as pltpu
 from jax.sharding import PartitionSpec as P
 
+
 LINE = 128
 MAXDY = 32
 EDGE = 8
+HALO = MAXDY + 2
 
 
 def rounded(rows):
@@ -61,15 +63,17 @@
 
 
 def relay_kernel(near, far, opposite, relay):
-    both = near.shape[1]
+    levels, both, width = near.shape
     slab = both // 2
     column = column_side()
     start = (1 - column) * (slab - EDGE)
     swapped = (column + layer_side()) % 2
+    row = lax.broadcasted_iota(jnp.int32, (levels, EDGE, width), 1)
+    low = (row < EDGE // 2) == (column == 1)
 
     def send(whole, partial):
         relay[:, :both] = whole[...]
-        relay[:, both:both + EDGE] = partial[:, aligned(start, EDGE)]
+        relay[:, both:] = jnp.where(low, partial[:, aligned(start, EDGE)], opposite[...])
 
     @pl.when(swapped == 0)
     def _():
@@ -78,8 +82,6 @@
     @pl.when(swapped == 1)
     def _():
         send(far, near)
-
-    relay[:, both + EDGE:] = opposite[...]
 
 
 def fill_whole(fine, coarse, fine_lines, coarse_lines):
@@ -107,12 +109,11 @@
             coarse_lines[line, :, aligned(coarse_center + slabs * slab, slab)] = (
                 piece[:, slab:both, lanes]
             )
-        for start, up in ((both, column), (both + EDGE, -column)):
-            row = below + (above - below) // 2 * (1 + up)
-            fine_lines[line, :, aligned(row, EDGE)] = relay[:, start:start + EDGE, lanes]
-
-
-def sweep_x_kernel(fill, shifts, fractions, *refs):
+        for row in (below, above):
+            fine_lines[line, :, row:row + EDGE] = relay[:, both:, lanes]
+
+
+def sweep_x_kernel(fill, shifts, _, fractions, *refs):
     *gathered, own, own_coarse, to_near, to_far, fine_lines, coarse_lines = refs
     lines, levels, _, _ = fine_lines.shape
     rows = own.shape[3]
@@ -141,13 +142,25 @@
                 lambda tap: coarse_lines[line, level, pl.ds(start + 2 - tap, slab)],
             )
     near_right = lax.axis_index("gy") % 2 == 0
+    half = LINE // 2
+    lane = lax.broadcasted_iota(jnp.int32, (rows, LINE), 1)
+    flat = lax.broadcasted_iota(jnp.int32, (slab // 2, LINE), 1)
     for level in range(levels):
-        leftward = own[0, 0, level], own[0, 1, level], own_coarse[0, level]
-        rightward = own[lines - 1, 1, level], own[lines - 1, 2, level], own_coarse[lines - 1, level]
-        for start, left, right in zip((0, rows, 2 * rows), leftward, rightward):
-            part = slice(start, start + left.shape[0])
-            to_near[level, part] = jnp.where(near_right, right, left)
-            to_far[level, part] = jnp.where(near_right, left, right)
+        last = lines - 1
+        left = jnp.where(
+            lane < LINE - HALO, own[0, 1, level], pltpu.roll(own[0, 0, level], LINE - HALO, 1)
+        )
+        right = jnp.where(
+            lane >= HALO, own[last, 1, level], pltpu.roll(own[last, 2, level], HALO, 1)
+        )
+        to_near[level, :rows] = jnp.where(near_right, right, left)
+        to_far[level, :rows] = jnp.where(near_right, left, right)
+        upper, lower = own_coarse[0, level, :slab // 2], own_coarse[0, level, slab // 2:]
+        left = jnp.where(flat < half, upper, pltpu.roll(lower, half, 1))
+        upper, lower = own_coarse[last, level, :slab // 2], own_coarse[last, level, slab // 2:]
+        right = jnp.where(flat < half, pltpu.roll(upper, half, 1), lower)
+        to_near[level, rows:] = jnp.where(near_right, right, left)
+        to_far[level, rows:] = jnp.where(near_right, left, right)
 
 
 def turned(weights, offset, current, left, right, lane):
@@ -179,23 +192,28 @@
     strip = lax.div(base, LINE)
     near_right = lax.axis_index("gy") % 2 == 0
 
-    def from_left(level, start, size):
-        part = slice(start, start + size)
-        return jnp.where(near_right, from_far[level, part], from_near[level, part])
-
-    def from_right(level, start, size):
-        part = slice(start, start + size)
-        return jnp.where(near_right, from_near[level, part], from_far[level, part])
+    def received(level):
+        near, far = from_near[level], from_far[level]
+        left, right = jnp.where(near_right, far, near), jnp.where(near_right, near, far)
+        half = LINE // 2
+        return {
+            "left": (left[:rows], pltpu.roll(left[:rows], LINE - HALO, 1)),
+            "right": (right[:rows], pltpu.roll(right[:rows], HALO, 1)),
+            "left_coarse": jnp.concatenate([pltpu.roll(left[rows:], half, 1), left[rows:]]),
+            "right_coarse": jnp.concatenate([right[rows:], pltpu.roll(right[rows:], half, 1)]),
+        }
+
+    halo = [received(level) for level in range(levels)]
 
     def pieces(region, level):
         if region < 0:
-            current = from_left(level, 0, rows)
+            current = halo[level]["left"][0]
             return current, current, own[0, 0, level]
         if region == lines:
-            current = from_right(level, rows, rows)
+            current = halo[level]["right"][0]
             return current, own[lines - 1, 2, level], current
-        left = own[region - 1, 2, level] if region else from_left(level, rows, rows)
-        right = own[region + 1, 0, level] if region < lines - 1 else from_right(level, 0, rows)
+        left = own[region - 1, 2, level] if region else halo[level]["left"][1]
+        right = own[region + 1, 0, level] if region < lines - 1 else halo[level]["right"][1]
         return own[region, 1, level], left, right
 
     outer = {}
@@ -227,10 +245,9 @@
                 outer_y, shifts_y[strip, 0], outer[line, level],
                 outer[line - 1, level], outer[line + 1, level], flat,
             )
-            left = own_coarse[line - 1, level] if line else from_left(level, 2 * rows, slab)
+            left = own_coarse[line - 1, level] if line else halo[level]["left_coarse"]
             right = (
-                own_coarse[line + 1, level] if line < lines - 1
-                else from_right(level, 2 * rows, slab)
+                own_coarse[line + 1, level] if line < lines - 1 else halo[level]["right_coarse"]
             )
             coarse_field = turned(
                 coarse_y, shifts_y[strip, 2], own_coarse[line, level], left, right, flat
@@ -273,7 +290,7 @@
         beside, near, opposite, far = lax.optimization_barrier((beside, near, opposite, far))
         relay = pl.pallas_call(
             relay_kernel,
-            out_shape=like((levels, 2 * slab + 2 * EDGE, width)),
+            out_shape=like((levels, 2 * slab + EDGE, width)),
             in_specs=on_chip(3),
             out_specs=on_chip(1)[0],
             compiler_params=params,
@@ -284,17 +301,17 @@
     else:
         fill = fill_whole
         gathered = ring_window(fine_cotangent, slabs_fine), ring_window(coarse_cotangent, slabs_coarse)
-    sent = like((levels, 2 * rows + slab, LINE))
+    sent = like((levels, rows + slab // 2, LINE))
     own, own_coarse, to_near, to_far = pl.pallas_call(
         functools.partial(sweep_x_kernel, fill),
         out_shape=[
             like((lines, 3, levels, rows, LINE)), like((lines, levels, slab, LINE)), sent, sent,
         ],
-        in_specs=scalars(2) + on_chip(len(gathered)),
+        in_specs=scalars(3) + on_chip(len(gathered)),
         out_specs=on_chip(4),
         scratch_shapes=windows,
         compiler_params=params,
-    )(upstream_x, fractions.T, *gathered)
+    )(upstream_x, upstream_y.T, fractions.T, *gathered)
     from_near = exchanged(to_near, "gy", lambda j: j ^ 1)
     from_far = exchanged(to_far, "gy", lambda j: (j - 1 + 2 * (j % 2)) % count_y)
     return pl.pallas_call(
@@ -309,6 +326,11 @@
 
 def solution(mesh):
     placed = (P(None, "gx", "gy"), P(None, "gx", "gy"), P(), P(), P())
-    return jax.shard_map(
-        local, mesh=mesh, in_specs=placed, out_specs=P(None, "gx", "gy"), check_vma=False
+
+    def step(*args):
+        return local(*args)
+
+    step = jax.shard_map(
+        step, mesh=mesh, in_specs=placed, out_specs=P(None, "gx", "gy"), check_vma=False
     )
+    return step

time: 23.7 us -> 23.2 us (0.979)
  waiting for transfers between devices: 8.93 us -> 8.3 us
    ppermute x7, waiting for transfers between devices: 8.93 us -> 8.3 us  [exchanged(): lax.ppermute(block, axis, [(i, partner(i)) for i in range(lax.axis_size(a...]
where the time goes in v3:
time: 23.2 us; the launch traced here: 23 us
  starting transfers between devices  10.8 us (47%)
  waiting for transfers between devices  8.3 us (36%)
  Pallas kernels  2.31 us (10%)
  other arithmetic  0.78 us (3%)
  local copies, waits for them, and re-layouts  0.69 us (3%)
    ppermute x7, starting transfers between devices, exchanged(): lax.ppermute(block, axis, [(i, partner(i)) for i in range(lax.axis_size(a...  10.8 us
    ppermute x7, waiting for transfers between devices, exchanged(): lax.ppermute(block, axis, [(i, partner(i)) for i in range(lax.axis_size(a...  8.3 us
    pallas_call x1, Pallas kernels, local(): pl.pallas_call(sweep_y_kernel, out_shape=like((levels, slab, width)), in_...  1.54 us
    concatenate x1, other arithmetic, local(): packed = jnp.concatenate([fine_cotangent, coarse_cotangent], axis=1)  0.78 us
    pallas_call x1, Pallas kernels, local(): pl.pallas_call(functools.partial(sweep_x_kernel, fill), out_shape=[like((...  0.73 us
    unnamed x6, local copies, waits for them, and re-layouts  0.68 us
  transfers between devices with their start and end apart: 7, of which 3 were waited for; matrix products, arithmetic and copies ran while one was open for 0% of the time, Pallas kernels for 0%

profile of v3, /device:TPU:1, one launch (start us, length us, event | category | flops | bytes accessed | tf_op | source)
XLA Modules:
  0.0 23.0 jit_solution(16158208194793284579)
XLA Ops:
  0.0 0.8 %pad_maximum_fusion.refs_0_ = f32[2,32,256]{2,1,0:T(8,128)S(1)} fusion(f32[2,16,256]{2,1,0:T(8,128)} %param.6, f32[2,16,256]{2,1,0:T(8,128)} %param.5), kind=kLoop, calls=%fused_computation | loop fusion | flops 16384 | bytes 131072 | tf_op jit(solution)/shard_map/concatenate | solution.py:283
  0.8 4.1 %collective-permute-start.3 = (f32[2,32,256]{2,1,0:T(8,128)S(1)}, f32[2,32,256]{2,1,0:T(8,128)S(1)}, u32[]{:S(2)}, u32[]{:S(2)}) collective-permute-start(f32[2,32,256]{2,1,0:T(8,128)S(1)} %pad_maximum_fusion.refs_0_), channel_id=1, source_target_pairs={{0,24},{4,28},{8,16},{12,20},{16,8},{20,12},{24,0},{28,4},{1,25},{... | collective-permute-start | bytes 196616 | tf_op jit(solution)/shard_map/ppermute | solution.py:22
  4.9 0.0 collective-permute-start.1
  4.9 1.2 %collective-permute-start = (f32[2,32,256]{2,1,0:T(8,128)S(1)}, f32[2,32,256]{2,1,0:T(8,128)S(1)}, u32[]{:S(2)}, u32[]{:S(2)}) collective-permute-start(f32[2,32,256]{2,1,0:T(8,128)S(1)} %pad_maximum_fusion.refs_0_), channel_id=1, source_target_pairs={{0,4},{4,0},{8,12},{12,8},{16,20},{20,16},{24,28},{28,24},{1,5},{5... | collective-permute-start | bytes 196616 | tf_op jit(solution)/shard_map/ppermute | solution.py:22
  6.1 0.4 %collective-permute-start.2 = (f32[2,8,256]{2,1,0:T(8,128)S(1)}, f32[2,8,256]{2,1,0:T(8,128)S(1)}, u32[]{:S(2)}, u32[]{:S(2)}) collective-permute-start(f32[2,8,256]{2,1,0:T(8,128)S(1)} %constant_dynamic-slice_fusion), channel_id=1, source_target_pairs={{0,16},{4,20},{8,24},{12,28},{16,0},{20,4},{24,8},{28,12},{1,17},{... | collective-permute-start | bytes 49160 | tf_op jit(solution)/shard_map/ppermute | solution.py:22
  6.5 3.1 %collective-permute-done.2.opposite = f32[2,8,256]{2,1,0:T(8,128)S(1)} collective-permute-done((f32[2,8,256]{2,1,0:T(8,128)S(1)}, f32[2,8,256]{2,1,0:T(8,128)S(1)}, u32[]{:S(2)}, u32[]{:S(2)}) %collective-permute-start.2) | collective-permute-done | bytes 16416 | tf_op jit(solution)/shard_map/ppermute | solution.py:22
  9.6 0.0 collective-permute-done.3.far.refs_3_
  9.6 0.0 collective-permute-done.1.near.refs_2_
  9.6 0.0 collective-permute-done.refs_1_
  9.7 0.0 copy-start
  9.7 0.3 %collective-permute-start.4 = (f32[2,40,256]{2,1,0:T(8,128)S(1)}, f32[2,40,256]{2,1,0:T(8,128)S(1)}, u32[]{:S(2)}, u32[]{:S(2)}) collective-permute-start(f32[2,40,256]{2,1,0:T(8,128)S(1)} %shard_map.55), channel_id=1, source_target_pairs={{0,4},{4,0},{8,12},{12,8},{16,20},{20,16},{24,28},{28,24},{1,5},{5... | collective-permute-start | bytes 245768 | tf_op jit(solution)/shard_map/ppermute | solution.py:22
  10.0 3.0 %collective-permute-done.4.refs_4_ = f32[2,40,256]{2,1,0:T(8,128)S(1)} collective-permute-done((f32[2,40,256]{2,1,0:T(8,128)S(1)}, f32[2,40,256]{2,1,0:T(8,128)S(1)}, u32[]{:S(2)}, u32[]{:S(2)}) %collective-permute-start.4) | collective-permute-done | bytes 81952 | tf_op jit(solution)/shard_map/ppermute | solution.py:22
  13.1 0.0 copy-start.1
  13.1 0.0 copy-start.2
  13.1 0.0 copy-done
  13.1 0.7 %copy-done.1 = f32[3,2]{0,1:T(2,128)S(1)} copy-done((f32[3,2]{0,1:T(2,128)S(1)}, f32[3,2]{0,1:T(2,128)}, u32[]{:S(2)}) %copy-start.1) | copy-done | bytes 48
  13.7 0.0 copy-done.2
  13.7 0.7 %shard_map.56 = (f32[2,3,2,24,128]{4,3,2,1,0:T(8,128)S(1)}, f32[2,2,16,128]{3,2,1,0:T(8,128)S(1)}, f32[2,32,128]{2,1,0:T(8,128)S(1)}, f32[2,32,128]{2,1,0:T(8,128)S(1)}) custom-call(s32[3,8]{1,0:T(4,128)S(1)} %copy-done, s32[1,3]{1,0:T(1,128)S(1)} %bitcast.4, f32[2,3]{1,0:T(2,128)S(1)} %bitcast.2, f32[2,32,256]{2,1,0:T(8,128)S(1)} %pad_maximum_fusion.refs_0_, ...), custom_call_target="tpu_custom_call" | custom-call | tf_op jit(solution)/shard_map/pallas_call | solution.py:305
  14.5 3.6 %collective-permute-start.5 = (f32[2,32,128]{2,1,0:T(8,128)S(1)}, f32[2,32,128]{2,1,0:T(8,128)S(1)}, u32[]{:S(2)}, u32[]{:S(2)}) collective-permute-start(f32[2,32,128]{2,1,0:T(8,128)S(1)} %get-tuple-element.19), channel_id=1, source_target_pairs={{0,1},{1,0},{2,3},{3,2},{4,5},{5,4},{6,7},{7,6},{8,9},{9,8},{10,11... | collective-permute-start | bytes 98312 | tf_op jit(solution)/shard_map/ppermute | solution.py:22
  18.1 1.2 %collective-permute-start.6 = (f32[2,32,128]{2,1,0:T(8,128)S(1)}, f32[2,32,128]{2,1,0:T(8,128)S(1)}, u32[]{:S(2)}, u32[]{:S(2)}) collective-permute-start(f32[2,32,128]{2,1,0:T(8,128)S(1)} %get-tuple-element.20), channel_id=1, source_target_pairs={{0,3},{1,2},{2,1},{3,0},{4,7},{5,6},{6,5},{7,4},{8,11},{9,10},{10,... | collective-permute-start | bytes 98312 | tf_op jit(solution)/shard_map/ppermute | solution.py:22
  19.3 0.0 collective-permute-done.5.from_near
  19.3 2.1 %collective-permute-done.6.from_far = f32[2,32,128]{2,1,0:T(8,128)S(1)} collective-permute-done((f32[2,32,128]{2,1,0:T(8,128)S(1)}, f32[2,32,128]{2,1,0:T(8,128)S(1)}, u32[]{:S(2)}, u32[]{:S(2)}) %collective-permute-start.6) | collective-permute-done | bytes 32800 | tf_op jit(solution)/shard_map/ppermute | solution.py:22
  21.4 1.5 %shard_map.57 = f32[2,16,256]{2,1,0:T(8,128)} custom-call(s32[3,8]{1,0:T(4,128)S(1)} %copy-done, s32[1,3]{1,0:T(1,128)S(1)} %bitcast.5, f32[2,3]{1,0:T(2,128)S(1)} %bitcast.3, f32[2,3,2,24,128]{4,3,2,1,0:T(8,128)S(1)} %get-tuple-element.17.own, f32[2,2,16,128]{3,2,1,0:T(8,128)S(1)} %get-tuple-element.18.own_coarse, ...), custom_call_target="tpu_custom_call" | custom-call | tf_op jit(solution)/shard_map/pallas_call | solution.py:317
  (2 shorter events, 0.0 us)
Async XLA Ops:
  0.8 8.8 %collective-permute-start.3 = (f32[2,32,256]{2,1,0:T(8,128)S(1)}, f32[2,32,256]{2,1,0:T(8,128)S(1)}, u32[]{:S(2)}, u32[]{:S(2)}) collective-permute-start(f32[2,32,256]{2,1,0:T(8,128)S(1)} %pad_maximum_fusion.refs_0_), channel_id=1, source_target_pairs={{0,24},{4,28},{8,16},{12,20},{16,8},{20,12},{24,0},{28,4},{1,25},{... | collective-permute-start | bytes 196616 | tf_op jit(solution)/shard_map/ppermute | solution.py:22
  4.9 4.7 %collective-permute-start.1 = (f32[2,32,256]{2,1,0:T(8,128)S(1)}, f32[2,32,256]{2,1,0:T(8,128)S(1)}, u32[]{:S(2)}, u32[]{:S(2)}) collective-permute-start(f32[2,32,256]{2,1,0:T(8,128)S(1)} %pad_maximum_fusion.refs_0_), channel_id=1, source_target_pairs={{0,8},{4,12},{8,0},{12,4},{16,24},{20,28},{24,16},{28,20},{1,9},{5... | collective-permute-start | bytes 196616 | tf_op jit(solution)/shard_map/ppermute | solution.py:22
  4.9 4.7 %collective-permute-start = (f32[2,32,256]{2,1,0:T(8,128)S(1)}, f32[2,32,256]{2,1,0:T(8,128)S(1)}, u32[]{:S(2)}, u32[]{:S(2)}) collective-permute-start(f32[2,32,256]{2,1,0:T(8,128)S(1)} %pad_maximum_fusion.refs_0_), channel_id=1, source_target_pairs={{0,4},{4,0},{8,12},{12,8},{16,20},{20,16},{24,28},{28,24},{1,5},{5... | collective-permute-start | bytes 196616 | tf_op jit(solution)/shard_map/ppermute | solution.py:22
  6.1 3.5 %collective-permute-start.2 = (f32[2,8,256]{2,1,0:T(8,128)S(1)}, f32[2,8,256]{2,1,0:T(8,128)S(1)}, u32[]{:S(2)}, u32[]{:S(2)}) collective-permute-start(f32[2,8,256]{2,1,0:T(8,128)S(1)} %constant_dynamic-slice_fusion), channel_id=1, source_target_pairs={{0,16},{4,20},{8,24},{12,28},{16,0},{20,4},{24,8},{28,12},{1,17},{... | collective-permute-start | bytes 49160 | tf_op jit(solution)/shard_map/ppermute | solution.py:22
  9.7 3.4 %copy-start = (s32[3,8]{1,0:T(4,128)S(1)}, s32[3,8]{1,0:T(4,128)}, u32[]{:S(2)}) copy-start(s32[3,8]{1,0:T(4,128)} %shifts_x.1) | copy-start | bytes 292
  9.7 3.4 %collective-permute-start.4 = (f32[2,40,256]{2,1,0:T(8,128)S(1)}, f32[2,40,256]{2,1,0:T(8,128)S(1)}, u32[]{:S(2)}, u32[]{:S(2)}) collective-permute-start(f32[2,40,256]{2,1,0:T(8,128)S(1)} %shard_map.55), channel_id=1, source_target_pairs={{0,4},{4,0},{8,12},{12,8},{16,20},{20,16},{24,28},{28,24},{1,5},{5... | collective-permute-start | bytes 245768 | tf_op jit(solution)/shard_map/ppermute | solution.py:22
  13.1 0.7 %copy-start.1 = (f32[3,2]{0,1:T(2,128)S(1)}, f32[3,2]{0,1:T(2,128)}, u32[]{:S(2)}) copy-start(f32[3,2]{0,1:T(2,128)} %param.9) | copy-start | bytes 76
  13.1 0.7 %copy-start.2 = (s32[3,1]{0,1:T(1,128)S(1)}, s32[3,1]{0,1:T(1,128)}, u32[]{:S(2)}) copy-start(s32[3,1]{0,1:T(1,128)} %param.8) | copy-start | bytes 40
  14.5 4.8 %collective-permute-start.5 = (f32[2,32,128]{2,1,0:T(8,128)S(1)}, f32[2,32,128]{2,1,0:T(8,128)S(1)}, u32[]{:S(2)}, u32[]{:S(2)}) collective-permute-start(f32[2,32,128]{2,1,0:T(8,128)S(1)} %get-tuple-element.19), channel_id=1, source_target_pairs={{0,1},{1,0},{2,3},{3,2},{4,5},{5,4},{6,7},{7,6},{8,9},{9,8},{10,11... | collective-permute-start | bytes 98312 | tf_op jit(solution)/shard_map/ppermute | solution.py:22
  18.1 3.3 %collective-permute-start.6 = (f32[2,32,128]{2,1,0:T(8,128)S(1)}, f32[2,32,128]{2,1,0:T(8,128)S(1)}, u32[]{:S(2)}, u32[]{:S(2)}) collective-permute-start(f32[2,32,128]{2,1,0:T(8,128)S(1)} %get-tuple-element.20), channel_id=1, source_target_pairs={{0,3},{1,2},{2,1},{3,0},{4,7},{5,6},{6,5},{7,4},{8,11},{9,10},{10,... | collective-permute-start | bytes 98312 | tf_op jit(solution)/shard_map/ppermute | solution.py:22

commit v4 on v3

--- a/solution.py
+++ b/solution.py
@@ -113,29 +113,65 @@
             fine_lines[line, :, row:row + EDGE] = relay[:, both:, lanes]
 
 
-def sweep_x_kernel(fill, shifts, _, fractions, *refs):
+def table_kernel(slab, lines, fine_center, coarse_center,
+                 shifts_x, shifts_y, fractions, offsets, weights):
+    total = shifts_x.shape[1]
+    strips = shifts_y.shape[0]
+    first = lax.axis_index("gy") * lines
+    base = lax.axis_index("gx") * slab
+    extent = lax.axis_size("gx") * slab
+    values = []
+    for line in range(lines):
+        inner = shifts_x[1, first + line]
+        for slot in range(3):
+            region = lax.rem(first + line + slot - 1 + total, total)
+            values.append(fine_center - 1 + inner + shifts_x[0, region])
+        values.append(coarse_center + shifts_x[2, first + line])
+    strip = lax.div(base, LINE)
+    values += [shifts_y[strip, 0], shifts_y[strip, 2]]
+    for region in range(-1, lines + 1):
+        shift = shifts_x[0, lax.rem(first + region + total, total)]
+        start = lax.rem(base + shift - 1 + extent, extent)
+        here = lax.div(start, LINE)
+        values += [
+            shifts_y[here, 1], shifts_y[lax.rem(here + 1, strips), 1], LINE - lax.rem(start, LINE)
+        ]
+    lane = lax.broadcasted_iota(jnp.int32, (1, LINE), 1)
+    row = jnp.zeros((1, LINE), jnp.int32)
+    for index, value in enumerate(values):
+        row = jnp.where(lane == index, value, row)
+    offsets[...] = row
+    for axis in range(2):
+        for level_pass in range(3):
+            taps = cubic_weights(fractions[axis, level_pass])
+            for tap, weight in enumerate(taps):
+                start = 4 * (3 * axis + level_pass) + tap
+                weights[start:start + 1] = jnp.full((1, LINE), weight, jnp.float32)
+
+
+def taps_of(weights, axis, level_pass):
+    start = 4 * (3 * axis + level_pass)
+    return [weights[start + tap:start + tap + 1] for tap in range(4)]
+
+
+def sweep_x_kernel(fill, offsets, weights, *refs):
     *gathered, own, own_coarse, to_near, to_far, fine_lines, coarse_lines = refs
     lines, levels, _, _ = fine_lines.shape
     rows = own.shape[3]
     slab = own_coarse.shape[2]
-    total = shifts.shape[1]
-    first = lax.axis_index("gy") * lines
-    fine_center = (fine_lines.shape[2] - slab) // 2
-    coarse_center = (coarse_lines.shape[2] - slab) // 2
-    fine_weights = cubic_weights(fractions[0, 1])
-    coarse_weights = cubic_weights(fractions[0, 2])
+    starts = offsets[...]
+    fine_weights = taps_of(weights, 0, 1)
+    coarse_weights = taps_of(weights, 0, 2)
     fill(*gathered, fine_lines, coarse_lines)
     for line in range(lines):
-        inner = shifts[1, first + line]
         for slot in range(3):
-            region = lax.rem(first + line + slot - 1 + total, total)
-            start = fine_center - 1 + inner + shifts[0, region]
+            start = starts[0, 4 * line + slot]
             for level in range(levels):
                 own[line, slot, level] = weighted(
                     fine_weights,
                     lambda tap: fine_lines[line, level, pl.ds(start + 2 - tap, rows)],
                 )
-        start = coarse_center + shifts[2, first + line]
+        start = starts[0, 4 * line + 3]
         for level in range(levels):
             own_coarse[line, level] = weighted(
                 coarse_weights,
@@ -175,22 +211,19 @@
     return weighted(weights, term)
 
 
-def sweep_y_kernel(shifts_x, shifts_y, fractions, own, own_coarse, from_near, from_far, out, held):
+def sweep_y_kernel(strips, offsets, weights, own, own_coarse, from_near, from_far, out, held):
     lines, _, levels, rows, _ = own.shape
     slab = own_coarse.shape[2]
-    total = shifts_x.shape[1]
-    strips = shifts_y.shape[0]
-    first = lax.axis_index("gy") * lines
-    base = lax.axis_index("gx") * slab
-    extent = lax.axis_size("gx") * slab
-    outer_x = cubic_weights(fractions[0, 0])
-    outer_y = cubic_weights(fractions[1, 0])
-    inner_y = cubic_weights(fractions[1, 1])
-    coarse_y = cubic_weights(fractions[1, 2])
+    outer_x = taps_of(weights, 0, 0)
+    outer_y = taps_of(weights, 1, 0)
+    inner_y = taps_of(weights, 1, 1)
+    coarse_y = taps_of(weights, 1, 2)
     tall = lax.broadcasted_iota(jnp.int32, (rows, LINE), 1)
     flat = lax.broadcasted_iota(jnp.int32, (slab, LINE), 1)
-    strip = lax.div(base, LINE)
+    row = lax.broadcasted_iota(jnp.int32, (rows, LINE), 0)
     near_right = lax.axis_index("gy") % 2 == 0
+    shifts = offsets[...]
+    outer_shift, coarse_shift = shifts[0, 4 * lines], shifts[0, 4 * lines + 1]
 
     def received(level):
         near, far = from_near[level], from_far[level]
@@ -218,23 +251,17 @@
 
     outer = {}
     for region in range(-1, lines + 1):
-        if strips > 1:
-            shift = shifts_x[0, lax.rem(first + region + total, total)]
-            start = lax.rem(base + shift - 1 + extent, extent)
-            here = lax.div(start, LINE)
-            after = lax.rem(here + 1, strips)
-            row = lax.broadcasted_iota(jnp.int32, (rows, LINE), 0)
-            beyond = row >= LINE - lax.rem(start, LINE)
+        entry = 4 * lines + 2 + (3 * (region + 1) if strips > 1 else 0)
+        here = shifts[0, entry]
         for level in range(levels):
             current, left, right = pieces(region, level)
+            swept = turned(inner_y, here, current, left, right, tall)
             if strips > 1:
                 swept = jnp.where(
-                    beyond,
-                    turned(inner_y, shifts_y[after, 1], current, left, right, tall),
-                    turned(inner_y, shifts_y[here, 1], current, left, right, tall),
+                    row >= shifts[0, entry + 2],
+                    turned(inner_y, shifts[0, entry + 1], current, left, right, tall),
+                    swept,
                 )
-            else:
-                swept = turned(inner_y, shifts_y[0, 1], current, left, right, tall)
             held[region + 1, level] = swept
             outer[region, level] = weighted(
                 outer_x, lambda tap: held[region + 1, level, 3 - tap:3 - tap + slab]
@@ -242,7 +269,7 @@
     for line in range(lines):
         for level in range(levels):
             fine_field = turned(
-                outer_y, shifts_y[strip, 0], outer[line, level],
+                outer_y, outer_shift, outer[line, level],
                 outer[line - 1, level], outer[line + 1, level], flat,
             )
             left = own_coarse[line - 1, level] if line else halo[level]["left_coarse"]
@@ -250,7 +277,7 @@
                 own_coarse[line + 1, level] if line < lines - 1 else halo[level]["right_coarse"]
             )
             coarse_field = turned(
-                coarse_y, shifts_y[strip, 2], own_coarse[line, level], left, right, flat
+                coarse_y, coarse_shift, own_coarse[line, level], left, right, flat
             )
             out[level, :, line * LINE:(line + 1) * LINE] = fine_field - coarse_field
 
@@ -279,6 +306,13 @@
     ]
     limit = (4 << 20) + 12 * levels * (slabs_fine + slabs_coarse + 1) * slab * width * 4
     params = pltpu.CompilerParams(vmem_limit_bytes=limit)
+    offsets, weights = pl.pallas_call(
+        functools.partial(table_kernel, slab, lines, slabs_fine * slab, slabs_coarse * slab),
+        out_shape=[jax.ShapeDtypeStruct((1, LINE), jnp.int32), like((4 * 6, LINE))],
+        in_specs=scalars(3),
+        out_specs=on_chip(2),
+        compiler_params=params,
+    )(upstream_x, upstream_y.T, fractions.T)
     if count_x == 8 and slab == 2 * EDGE:
         packed = jnp.concatenate([fine_cotangent, coarse_cotangent], axis=1)
         packed = lax.optimization_barrier(packed)
@@ -307,21 +341,21 @@
         out_shape=[
             like((lines, 3, levels, rows, LINE)), like((lines, levels, slab, LINE)), sent, sent,
         ],
-        in_specs=scalars(3) + on_chip(len(gathered)),
+        in_specs=on_chip(2 + len(gathered)),
         out_specs=on_chip(4),
         scratch_shapes=windows,
         compiler_params=params,
-    )(upstream_x, upstream_y.T, fractions.T, *gathered)
+    )(offsets, weights, *gathered)
     from_near = exchanged(to_near, "gy", lambda j: j ^ 1)
     from_far = exchanged(to_far, "gy", lambda j: (j - 1 + 2 * (j % 2)) % count_y)
     return pl.pallas_call(
-        sweep_y_kernel,
+        functools.partial(sweep_y_kernel, upstream_y.shape[1]),
         out_shape=like((levels, slab, width)),
-        in_specs=scalars(3) + on_chip(4),
+        in_specs=on_chip(6),
         out_specs=on_chip(1)[0],
         scratch_shapes=[pltpu.VMEM((lines + 2, levels, rows, LINE), fine_cotangent.dtype)],
         compiler_params=params,
-    )(upstream_x, upstream_y.T, fractions.T, own, own_coarse, from_near, from_far)
+    )(offsets, weights, own, own_coarse, from_near, from_far)
 
 
 def solution(mesh):

time: 23.2 us -> 21.5 us (0.927)
  waiting for transfers between devices: 8.3 us -> 6.94 us
  Pallas kernels: 2.31 us -> 1.95 us
    ppermute x7, waiting for transfers between devices: 8.3 us -> 6.94 us  [exchanged(): lax.ppermute(block, axis, [(i, partner(i)) for i in range(lax.axis_size(a...]
    pallas_call x1, Pallas kernels: 0.73 us -> 0.21 us  [local(): pl.pallas_call(functools.partial(sweep_x_kernel, fill), out_shape=[like((...]
    pallas_call x1 -> x2, Pallas kernels: 1.54 us -> 1.7 us  [the longest x1 1.03 us: local(): pl.pallas_call(functools.partial(sweep_y_kernel, upstream_y.shape[1]), ou...]
  transfers between devices with their start and end apart: 7 -> 7, of which waited for: 3 -> 3; matrix products, arithmetic and copies ran while one was open for 0% -> 0% of each run, Pallas kernels for 0% -> 3%
where the time goes in v4:
time: 21.5 us; the launch traced here: 21.2 us
  starting transfers between devices  10.8 us (50%)
  waiting for transfers between devices  6.94 us (32%)
  Pallas kernels  1.95 us (9%)
  other arithmetic  0.78 us (4%)
  local copies, waits for them, and re-layouts  0.69 us (3%)
    ppermute x7, starting transfers between devices, exchanged(): lax.ppermute(block, axis, [(i, partner(i)) for i in range(lax.axis_size(a...  10.8 us
    ppermute x7, waiting for transfers between devices, exchanged(): lax.ppermute(block, axis, [(i, partner(i)) for i in range(lax.axis_size(a...  6.94 us
    pallas_call x1, Pallas kernels, local(): pl.pallas_call(functools.partial(sweep_y_kernel, upstream_y.shape[1]), ou...  1.03 us
    concatenate x1, other arithmetic, local(): packed = jnp.concatenate([fine_cotangent, coarse_cotangent], axis=1)  0.78 us
    unnamed x6, local copies, waits for them, and re-layouts  0.68 us
    pallas_call x1, Pallas kernels, local(): pl.pallas_call(functools.partial(table_kernel, slab, lines, slabs_fine *...  0.67 us
  transfers between devices with their start and end apart: 7, of which 3 were waited for; matrix products, arithmetic and copies ran while one was open for 0% of the time, Pallas kernels for 3%

profile of v4, /device:TPU:1, one launch (start us, length us, event | category | flops | bytes accessed | tf_op | source)
XLA Modules:
  0.0 21.2 jit_solution(11097472803531318038)
XLA Ops:
  0.0 0.8 %pad_maximum_fusion.refs_0_ = f32[2,32,256]{2,1,0:T(8,128)S(1)} fusion(f32[2,16,256]{2,1,0:T(8,128)} %param.6, f32[2,16,256]{2,1,0:T(8,128)} %param.5), kind=kLoop, calls=%fused_computation | loop fusion | flops 16384 | bytes 131072 | tf_op jit(solution)/shard_map/concatenate | solution.py:317
  0.8 4.1 %collective-permute-start.3 = (f32[2,32,256]{2,1,0:T(8,128)S(1)}, f32[2,32,256]{2,1,0:T(8,128)S(1)}, u32[]{:S(2)}, u32[]{:S(2)}) collective-permute-start(f32[2,32,256]{2,1,0:T(8,128)S(1)} %pad_maximum_fusion.refs_0_), channel_id=1, source_target_pairs={{0,24},{4,28},{8,16},{12,20},{16,8},{20,12},{24,0},{28,4},{1,25},{... | collective-permute-start | bytes 196616 | tf_op jit(solution)/shard_map/ppermute | solution.py:22
  4.9 0.0 collective-permute-start.1
  4.9 1.2 %collective-permute-start = (f32[2,32,256]{2,1,0:T(8,128)S(1)}, f32[2,32,256]{2,1,0:T(8,128)S(1)}, u32[]{:S(2)}, u32[]{:S(2)}) collective-permute-start(f32[2,32,256]{2,1,0:T(8,128)S(1)} %pad_maximum_fusion.refs_0_), channel_id=1, source_target_pairs={{0,4},{4,0},{8,12},{12,8},{16,20},{20,16},{24,28},{28,24},{1,5},{5... | collective-permute-start | bytes 196616 | tf_op jit(solution)/shard_map/ppermute | solution.py:22
  6.1 0.4 %collective-permute-start.2 = (f32[2,8,256]{2,1,0:T(8,128)S(1)}, f32[2,8,256]{2,1,0:T(8,128)S(1)}, u32[]{:S(2)}, u32[]{:S(2)}) collective-permute-start(f32[2,8,256]{2,1,0:T(8,128)S(1)} %constant_dynamic-slice_fusion), channel_id=1, source_target_pairs={{0,16},{4,20},{8,24},{12,28},{16,0},{20,4},{24,8},{28,12},{1,17},{... | collective-permute-start | bytes 49160 | tf_op jit(solution)/shard_map/ppermute | solution.py:22
  6.5 3.1 %collective-permute-done.2.opposite = f32[2,8,256]{2,1,0:T(8,128)S(1)} collective-permute-done((f32[2,8,256]{2,1,0:T(8,128)S(1)}, f32[2,8,256]{2,1,0:T(8,128)S(1)}, u32[]{:S(2)}, u32[]{:S(2)}) %collective-permute-start.2) | collective-permute-done | bytes 16416 | tf_op jit(solution)/shard_map/ppermute | solution.py:22
  9.6 0.0 collective-permute-done.3.far.refs_3_
  9.6 0.0 collective-permute-done.1.near.refs_2_
  9.6 0.0 collective-permute-done.refs_1_
  9.7 0.0 copy-start
  9.7 0.3 %collective-permute-start.4 = (f32[2,40,256]{2,1,0:T(8,128)S(1)}, f32[2,40,256]{2,1,0:T(8,128)S(1)}, u32[]{:S(2)}, u32[]{:S(2)}) collective-permute-start(f32[2,40,256]{2,1,0:T(8,128)S(1)} %shard_map.56), channel_id=1, source_target_pairs={{0,4},{4,0},{8,12},{12,8},{16,20},{20,16},{24,28},{28,24},{1,5},{5... | collective-permute-start | bytes 245768 | tf_op jit(solution)/shard_map/ppermute | solution.py:22
  10.0 0.0 copy-start.1
  10.0 0.0 copy-start.2
  10.0 0.3 %copy-done = s32[3,8]{1,0:T(4,128)S(1)} copy-done((s32[3,8]{1,0:T(4,128)S(1)}, s32[3,8]{1,0:T(4,128)}, u32[]{:S(2)}) %copy-start) | copy-done | bytes 120
  10.4 0.3 %copy-done.1 = f32[3,2]{0,1:T(2,128)S(1)} copy-done((f32[3,2]{0,1:T(2,128)S(1)}, f32[3,2]{0,1:T(2,128)}, u32[]{:S(2)}) %copy-start.1) | copy-done | bytes 48
  10.7 0.0 copy-done.2
  10.7 0.7 %shard_map.55 = (s32[1,128]{1,0:T(1,128)S(1)}, f32[24,128]{1,0:T(8,128)S(1)}) custom-call(s32[3,8]{1,0:T(4,128)S(1)} %copy-done, s32[1,3]{1,0:T(1,128)S(1)} %bitcast.3, f32[2,3]{1,0:T(2,128)S(1)} %bitcast.2), custom_call_target="tpu_custom_call" | custom-call | tf_op jit(solution)/shard_map/pallas_call | solution.py:309
  11.4 1.7 %collective-permute-done.4.refs_4_ = f32[2,40,256]{2,1,0:T(8,128)S(1)} collective-permute-done((f32[2,40,256]{2,1,0:T(8,128)S(1)}, f32[2,40,256]{2,1,0:T(8,128)S(1)}, u32[]{:S(2)}, u32[]{:S(2)}) %collective-permute-start.4) | collective-permute-done | bytes 81952 | tf_op jit(solution)/shard_map/ppermute | solution.py:22
  13.1 0.2 %shard_map.57 = (f32[2,3,2,24,128]{4,3,2,1,0:T(8,128)S(1)}, f32[2,2,16,128]{3,2,1,0:T(8,128)S(1)}, f32[2,32,128]{2,1,0:T(8,128)S(1)}, f32[2,32,128]{2,1,0:T(8,128)S(1)}) custom-call(s32[1,128]{1,0:T(1,128)S(1)} %get-tuple-element.15.offsets, f32[24,128]{1,0:T(8,128)S(1)} %get-tuple-element.16.weights, f32[2,32,256]{2,1,0:T(8,128)S(1)} %pad_maximum_fusion.refs_0_, ...), custom_call_target="tpu_custom_call" | custom-call | tf_op jit(solution)/shard_map/pallas_call | solution.py:339
  13.3 3.6 %collective-permute-start.5 = (f32[2,32,128]{2,1,0:T(8,128)S(1)}, f32[2,32,128]{2,1,0:T(8,128)S(1)}, u32[]{:S(2)}, u32[]{:S(2)}) collective-permute-start(f32[2,32,128]{2,1,0:T(8,128)S(1)} %get-tuple-element.23), channel_id=1, source_target_pairs={{0,1},{1,0},{2,3},{3,2},{4,5},{5,4},{6,7},{7,6},{8,9},{9,8},{10,11... | collective-permute-start | bytes 98312 | tf_op jit(solution)/shard_map/ppermute | solution.py:22
  16.9 1.2 %collective-permute-start.6 = (f32[2,32,128]{2,1,0:T(8,128)S(1)}, f32[2,32,128]{2,1,0:T(8,128)S(1)}, u32[]{:S(2)}, u32[]{:S(2)}) collective-permute-start(f32[2,32,128]{2,1,0:T(8,128)S(1)} %get-tuple-element.24), channel_id=1, source_target_pairs={{0,3},{1,2},{2,1},{3,0},{4,7},{5,6},{6,5},{7,4},{8,11},{9,10},{10,... | collective-permute-start | bytes 98312 | tf_op jit(solution)/shard_map/ppermute | solution.py:22
  18.1 0.0 collective-permute-done.5.from_near
  18.1 2.1 %collective-permute-done.6.from_far = f32[2,32,128]{2,1,0:T(8,128)S(1)} collective-permute-done((f32[2,32,128]{2,1,0:T(8,128)S(1)}, f32[2,32,128]{2,1,0:T(8,128)S(1)}, u32[]{:S(2)}, u32[]{:S(2)}) %collective-permute-start.6) | collective-permute-done | bytes 32800 | tf_op jit(solution)/shard_map/ppermute | solution.py:22
  20.2 1.0 %shard_map.58 = f32[2,16,256]{2,1,0:T(8,128)} custom-call(s32[1,128]{1,0:T(1,128)S(1)} %get-tuple-element.15.offsets, f32[24,128]{1,0:T(8,128)S(1)} %get-tuple-element.16.weights, f32[2,3,2,24,128]{4,3,2,1,0:T(8,128)S(1)} %get-tuple-element.21.own, f32[2,2,16,128]{3,2,1,0:T(8,128)S(1)} %get-tuple-element.22.own_coarse, ...), custom_call_target="tpu_custom_call" | custom-call | tf_op jit(solution)/shard_map/pallas_call | solution.py:351
  (2 shorter events, 0.0 us)
Async XLA Ops:
  0.8 8.8 %collective-permute-start.3 = (f32[2,32,256]{2,1,0:T(8,128)S(1)}, f32[2,32,256]{2,1,0:T(8,128)S(1)}, u32[]{:S(2)}, u32[]{:S(2)}) collective-permute-start(f32[2,32,256]{2,1,0:T(8,128)S(1)} %pad_maximum_fusion.refs_0_), channel_id=1, source_target_pairs={{0,24},{4,28},{8,16},{12,20},{16,8},{20,12},{24,0},{28,4},{1,25},{... | collective-permute-start | bytes 196616 | tf_op jit(solution)/shard_map/ppermute | solution.py:22
  4.9 4.7 %collective-permute-start.1 = (f32[2,32,256]{2,1,0:T(8,128)S(1)}, f32[2,32,256]{2,1,0:T(8,128)S(1)}, u32[]{:S(2)}, u32[]{:S(2)}) collective-permute-start(f32[2,32,256]{2,1,0:T(8,128)S(1)} %pad_maximum_fusion.refs_0_), channel_id=1, source_target_pairs={{0,8},{4,12},{8,0},{12,4},{16,24},{20,28},{24,16},{28,20},{1,9},{5... | collective-permute-start | bytes 196616 | tf_op jit(solution)/shard_map/ppermute | solution.py:22
  4.9 4.7 %collective-permute-start = (f32[2,32,256]{2,1,0:T(8,128)S(1)}, f32[2,32,256]{2,1,0:T(8,128)S(1)}, u32[]{:S(2)}, u32[]{:S(2)}) collective-permute-start(f32[2,32,256]{2,1,0:T(8,128)S(1)} %pad_maximum_fusion.refs_0_), channel_id=1, source_target_pairs={{0,4},{4,0},{8,12},{12,8},{16,20},{20,16},{24,28},{28,24},{1,5},{5... | collective-permute-start | bytes 196616 | tf_op jit(solution)/shard_map/ppermute | solution.py:22
  6.1 3.5 %collective-permute-start.2 = (f32[2,8,256]{2,1,0:T(8,128)S(1)}, f32[2,8,256]{2,1,0:T(8,128)S(1)}, u32[]{:S(2)}, u32[]{:S(2)}) collective-permute-start(f32[2,8,256]{2,1,0:T(8,128)S(1)} %constant_dynamic-slice_fusion), channel_id=1, source_target_pairs={{0,16},{4,20},{8,24},{12,28},{16,0},{20,4},{24,8},{28,12},{1,17},{... | collective-permute-start | bytes 49160 | tf_op jit(solution)/shard_map/ppermute | solution.py:22
  9.7 0.7 %copy-start = (s32[3,8]{1,0:T(4,128)S(1)}, s32[3,8]{1,0:T(4,128)}, u32[]{:S(2)}) copy-start(s32[3,8]{1,0:T(4,128)} %shifts_x.1) | copy-start | bytes 292
  9.7 3.4 %collective-permute-start.4 = (f32[2,40,256]{2,1,0:T(8,128)S(1)}, f32[2,40,256]{2,1,0:T(8,128)S(1)}, u32[]{:S(2)}, u32[]{:S(2)}) collective-permute-start(f32[2,40,256]{2,1,0:T(8,128)S(1)} %shard_map.56), channel_id=1, source_target_pairs={{0,4},{4,0},{8,12},{12,8},{16,20},{20,16},{24,28},{28,24},{1,5},{5... | collective-permute-start | bytes 245768 | tf_op jit(solution)/shard_map/ppermute | solution.py:22
  10.0 0.7 %copy-start.1 = (f32[3,2]{0,1:T(2,128)S(1)}, f32[3,2]{0,1:T(2,128)}, u32[]{:S(2)}) copy-start(f32[3,2]{0,1:T(2,128)} %param.9) | copy-start | bytes 76
  10.0 0.7 %copy-start.2 = (s32[3,1]{0,1:T(1,128)S(1)}, s32[3,1]{0,1:T(1,128)}, u32[]{:S(2)}) copy-start(s32[3,1]{0,1:T(1,128)} %param.8) | copy-start | bytes 40
  13.3 4.8 %collective-permute-start.5 = (f32[2,32,128]{2,1,0:T(8,128)S(1)}, f32[2,32,128]{2,1,0:T(8,128)S(1)}, u32[]{:S(2)}, u32[]{:S(2)}) collective-permute-start(f32[2,32,128]{2,1,0:T(8,128)S(1)} %get-tuple-element.23), channel_id=1, source_target_pairs={{0,1},{1,0},{2,3},{3,2},{4,5},{5,4},{6,7},{7,6},{8,9},{9,8},{10,11... | collective-permute-start | bytes 98312 | tf_op jit(solution)/shard_map/ppermute | solution.py:22
  16.9 3.3 %collective-permute-start.6 = (f32[2,32,128]{2,1,0:T(8,128)S(1)}, f32[2,32,128]{2,1,0:T(8,128)S(1)}, u32[]{:S(2)}, u32[]{:S(2)}) collective-permute-start(f32[2,32,128]{2,1,0:T(8,128)S(1)} %get-tuple-element.24), channel_id=1, source_target_pairs={{0,3},{1,2},{2,1},{3,0},{4,7},{5,6},{6,5},{7,4},{8,11},{9,10},{10,... | collective-permute-start | bytes 98312 | tf_op jit(solution)/shard_map/ppermute | solution.py:22
